TPU v7x, 32 devices: a whole 2x2x4 slice. The times are simulated.
32 devices in a mesh: shard: 4 (over y, x), replica: 8 (over z, core).
Axes of the slice: x: 2, y: 2, z: 4, core: 2. Of those that a mesh axis runs over, the one named last changes fastest.
Arguments:
- images: float32 [32, 197, 384], P(('shard', 'replica')), may hold values from -6 to 6
- cotangent: float32 [32, 197, 384], P(('shard', 'replica')), may hold values from -6 to 6
- counts: int32 [32], P(('shard', 'replica')), may hold values from 0 to 1, as said below
- w_qkv: bfloat16 [2, 384, 1152], P(None, 'shard'), may hold values from -0.3125 to 0.3125
- w_out: bfloat16 [2, 384, 384], P(None, 'shard'), may hold values from -1.25 to 1.25
- w_up: bfloat16 [2, 384, 1536], P(None, 'shard'), may hold values from -0.3125 to 0.3125
- w_down: bfloat16 [2, 1536, 384], P(None, 'shard'), may hold values from -0.15625 to 0.15625
- gains: bfloat16 [2, 2, 384], P(None, None, 'shard'), may hold values from 0.25 to 1.75
- biases: bfloat16 [2, 6, 384], P(None, None, 'shard'), may hold values from -1.796875 to 1.796875
- up_bias: bfloat16 [2, 1536], P(None, 'shard'), may hold values from -1.796875 to 1.796875
Outputs:
- activations: float32 [32, 197, 384], P(('shard', 'replica'))
- input_grad: float32 [32, 197, 384], P(('shard', 'replica'))
- grad_qkv: float32 [2, 384, 1152], P(None, 'shard')
- grad_out: float32 [2, 384, 384], P(None, 'shard')
- grad_up: float32 [2, 384, 1536], P(None, 'shard')
- grad_down: float32 [2, 1536, 384], P(None, 'shard')
- grad_gains: float32 [2, 2, 384], P(None, None, 'shard')
- grad_biases: float32 [2, 6, 384], P(None, None, 'shard')
- grad_upbias: float32 [2, 1536], P(None, 'shard')
Inputs may be any that keep to these rules, and one draw needn't show every extreme that they name: `counts`: some device has all 1 slots live and some other device has none.
All inputs are finite; a program needn't handle non-finite values.
Results may differ from a plain program's by a relative error of at most 0.018.
Values may be sent and summed in bfloat16 or wider, within the bound.
A program may use at most 128 MiB of HBM per device.

v0:
```python
import jax
import jax.numpy as jnp
from jax import lax
from jax.sharding import PartitionSpec as P

D = 384
HEADS = 6
HD = 64
S = 197
LAYERS = 2


EPS = 1e-06
INV_ROOT_TWO = 0.7071067811865476
INV_ROOT_TWO_PI = 0.3989422804014327


def normalize(values, gain, shift):
    center = jnp.mean(values, -1, keepdims=True)
    centered = values - center
    spread = jnp.mean(centered * centered, -1, keepdims=True)
    inverse = lax.rsqrt(spread + EPS)
    unit = centered * inverse
    return (unit * gain + shift, unit, inverse)


def norm_back(upstream, unit, inverse, gain):
    scaled = upstream * gain
    inner = (
        scaled
        - jnp.mean(scaled, -1, keepdims=True)
        - unit * jnp.mean(scaled * unit, -1, keepdims=True)
    )
    return (inverse * inner, jnp.sum(upstream * unit, 0), jnp.sum(upstream, 0))


def normal_cdf(values):
    return 0.5 * (1.0 + jax.scipy.special.erf(values * INV_ROOT_TWO))


def product(left, right):
    return jnp.dot(left, right, preferred_element_type=jnp.float32)


def product_left(left, right):
    return lax.dot_general(
        left, right, (((0,), (0,)), ((), ())), preferred_element_type=jnp.float32
    )


def product_right(left, right):
    return lax.dot_general(
        left, right, (((1,), (1,)), ((), ())), preferred_element_type=jnp.float32
    )


def batched(form, left, right):
    return jnp.einsum(form, left, right, preferred_element_type=jnp.float32)


def forward_layer(stream, params):
    w_qkv, w_out, w_up, w_down, gains, biases, up_bias = params
    gains = gains.astype(jnp.float32)
    biases = biases.astype(jnp.float32)
    up_bias = up_bias.astype(jnp.float32)
    blocks = stream.shape[0]
    factor = HD ** (-0.5)
    rows_in = stream.reshape(-1, D)
    normed_f, unit_one, scale_one = normalize(rows_in, gains[0], biases[0])
    normed_one = normed_f.astype(jnp.bfloat16)
    project = product(normed_one, w_qkv)
    queries = (
        ((project[:, :D] + biases[1]) * factor).astype(jnp.bfloat16).reshape(blocks, S, HEADS, HD)
    )
    key_rows = project[:, D : 2 * D].astype(jnp.bfloat16).reshape(blocks, S, HEADS, HD)
    values = (project[:, 2 * D :] + biases[2]).astype(jnp.bfloat16).reshape(blocks, S, HEADS, HD)
    scores = batched("bqhe,bkhe->bhqk", queries, key_rows)
    log_total = jnp.log(jnp.sum(jnp.exp(scores), -1, keepdims=True))
    probs = jnp.exp(scores - log_total)
    prob_low = probs.astype(jnp.bfloat16)
    mixed = batched("bhqk,bkhe->bqhe", prob_low, values).reshape(-1, D).astype(jnp.bfloat16)
    middle = rows_in + product(mixed, w_out) + biases[3]
    normed_g, unit_two, scale_two = normalize(middle, gains[1], biases[4])
    normed_two = normed_g.astype(jnp.bfloat16)
    hidden = product(normed_two, w_up) + up_bias
    activated = (hidden * normal_cdf(hidden)).astype(jnp.bfloat16)
    result = middle + product(activated, w_down) + biases[5]
    saved = (
        normed_one,
        unit_one,
        scale_one,
        queries,
        key_rows,
        values,
        log_total,
        mixed,
        normed_two,
        unit_two,
        scale_two,
        hidden,
        activated,
    )
    return (result.reshape(stream.shape), saved)


def backward_layer(saved, grad, params):
    w_qkv, w_out, w_up, w_down, gains, biases, up_bias = params
    gains_f = gains.astype(jnp.float32)
    factor = HD ** (-0.5)
    (
        normed_one,
        unit_one,
        scale_one,
        queries,
        key_rows,
        values,
        log_total,
        mixed,
        normed_two,
        unit_two,
        scale_two,
        hidden,
        activated,
    ) = saved
    blocks = queries.shape[0]
    low = grad.astype(jnp.bfloat16)
    down_grad = product_left(activated, low)
    shift_five = jnp.sum(grad, 0)
    act_grad = product_right(low, w_down)
    dens = jnp.exp(-0.5 * hidden * hidden) * INV_ROOT_TWO_PI
    hid_grad = act_grad * (normal_cdf(hidden) + hidden * dens)
    hid_low = hid_grad.astype(jnp.bfloat16)
    up_grad = product_left(normed_two, hid_low)
    upbias_grad = jnp.sum(hid_grad, 0)
    norm_grad = product_right(hid_low, w_up)
    back_two, gain_two, shift_four = norm_back(norm_grad, unit_two, scale_two, gains_f[1])
    mid_grad = grad + back_two
    mid_low = mid_grad.astype(jnp.bfloat16)
    out_grad = product_left(mixed, mid_low)
    shift_three = jnp.sum(mid_grad, 0)
    mixed_grad = product_right(mid_low, w_out).astype(jnp.bfloat16).reshape(blocks, S, HEADS, HD)
    scores = batched("bqhe,bkhe->bhqk", queries, key_rows)
    probs = jnp.exp(scores - log_total)
    prob_low = probs.astype(jnp.bfloat16)
    prob_grad = batched("bqhe,bkhe->bhqk", mixed_grad, values)
    row_dot = jnp.sum(probs * prob_grad, -1, keepdims=True)
    score_grad = (probs * (prob_grad - row_dot)).astype(jnp.bfloat16)
    query_grad = (batched("bhqk,bkhe->bqhe", score_grad, key_rows) * factor).reshape(-1, D)
    key_grad = batched("bhqk,bqhe->bkhe", score_grad, queries).reshape(-1, D)
    value_grad = batched("bhqk,bqhe->bkhe", prob_low, mixed_grad).reshape(-1, D)
    project_grad = jnp.concatenate([query_grad, key_grad, value_grad], 1).astype(jnp.bfloat16)
    qkv_grad = product_left(normed_one, project_grad)
    first_grad = product_right(project_grad, w_qkv)
    back_one, gain_one, shift_zero = norm_back(first_grad, unit_one, scale_one, gains_f[0])
    stream_grad = mid_grad + back_one
    grads = (
        qkv_grad,
        out_grad,
        up_grad,
        down_grad,
        jnp.stack([gain_one, gain_two], 0),
        jnp.stack(
            [
                shift_zero,
                jnp.sum(query_grad, 0),
                jnp.sum(value_grad, 0),
                shift_three,
                shift_four,
                shift_five,
            ],
            0,
        ),
        upbias_grad,
    )
    return (stream_grad, grads)


def fetch_forward(pieces):
    return (
        lax.all_gather(pieces[0], "shard", axis=0, tiled=True),
        lax.all_gather(pieces[1], "shard", axis=0, tiled=True),
        lax.all_gather(pieces[2], "shard", axis=0, tiled=True),
        lax.all_gather(pieces[3], "shard", axis=0, tiled=True),
        lax.all_gather(pieces[4], "shard", axis=1, tiled=True),
        lax.all_gather(pieces[5], "shard", axis=1, tiled=True),
        lax.all_gather(pieces[6], "shard", axis=0, tiled=True),
    )


def fetch_backward(pieces):
    return (
        lax.all_gather(pieces[0], "shard", axis=0, tiled=True),
        lax.all_gather(pieces[1], "shard", axis=0, tiled=True),
        lax.all_gather(pieces[2], "shard", axis=0, tiled=True),
        lax.all_gather(pieces[3], "shard", axis=0, tiled=True),
        lax.all_gather(pieces[4], "shard", axis=1, tiled=True),
        lax.all_gather(pieces[5], "shard", axis=1, tiled=True),
        lax.all_gather(pieces[6], "shard", axis=0, tiled=True),
    )


def reduce_layer(grads):
    owned = (
        lax.psum_scatter(
            grads[0].astype(jnp.bfloat16), "shard", scatter_dimension=0, tiled=True
        ).astype(jnp.float32),
        lax.psum_scatter(
            grads[1].astype(jnp.bfloat16), "shard", scatter_dimension=0, tiled=True
        ).astype(jnp.float32),
        lax.psum_scatter(
            grads[2].astype(jnp.bfloat16), "shard", scatter_dimension=0, tiled=True
        ).astype(jnp.float32),
        lax.psum_scatter(
            grads[3].astype(jnp.bfloat16), "shard", scatter_dimension=0, tiled=True
        ).astype(jnp.float32),
        lax.psum_scatter(
            grads[4].astype(jnp.bfloat16), "shard", scatter_dimension=1, tiled=True
        ).astype(jnp.float32),
        lax.psum_scatter(
            grads[5].astype(jnp.bfloat16), "shard", scatter_dimension=1, tiled=True
        ).astype(jnp.float32),
        lax.psum_scatter(
            grads[6].astype(jnp.bfloat16), "shard", scatter_dimension=0, tiled=True
        ).astype(jnp.float32),
    )
    return lax.psum(
        (owned[0], owned[1], owned[2], owned[3], owned[4], owned[5], owned[6]), "replica"
    )


def on_device(images, cotangent, counts, w_qkv, w_out, w_up, w_down, gains, biases, up_bias):
    stacks = (w_qkv, w_out, w_up, w_down, gains, biases, up_bias)
    slot_count = images.shape[0]
    live = (jnp.arange(slot_count, dtype=jnp.int32) < counts[0]).astype(jnp.float32)[:, None, None]
    held = []
    kept = []
    stream = images
    for layer in range(LAYERS):
        params = fetch_forward(tuple((stack[layer] for stack in stacks)))
        held.append(params)
        result, saved = forward_layer(stream, params)
        kept.append(saved)
        stream = result
    activations = stream * live
    grad = (cotangent * live).reshape(-1, D)
    reduced = [None] * LAYERS
    for layer in reversed(range(LAYERS)):
        params = fetch_backward(tuple((stack[layer] for stack in stacks)))
        grad, grads = backward_layer(kept[layer], grad, params)
        reduced[layer] = reduce_layer(grads)
    totals = tuple((jnp.stack([piece[index] for piece in reduced], 0) for index in range(7)))
    input_grad = grad.reshape(images.shape)
    return (
        activations,
        input_grad,
        totals[0],
        totals[1],
        totals[2],
        totals[3],
        totals[4],
        totals[5],
        totals[6],
    )


def solution(mesh):
    in_specs = (
        P(("shard", "replica"), None, None),
        P(("shard", "replica"), None, None),
        P(("shard", "replica")),
        P(None, "shard", None),
        P(None, "shard", None),
        P(None, "shard", None),
        P(None, "shard", None),
        P(None, None, "shard"),
        P(None, None, "shard"),
        P(None, "shard"),
    )
    out_specs = (
        P(("shard", "replica"), None, None),
        P(("shard", "replica"), None, None),
        P(None, "shard", None),
        P(None, "shard", None),
        P(None, "shard", None),
        P(None, "shard", None),
        P(None, None, "shard"),
        P(None, None, "shard"),
        P(None, "shard"),
    )
    return jax.shard_map(
        on_device, mesh=mesh, in_specs=in_specs, out_specs=out_specs, check_vma=False
    )
```

profile of v0, /device:TPU:0, one launch (start us, length us, event | category | flops | bytes accessed | tf_op | source)
XLA Modules:
  0.0 623.5 jit_solution(522053649379360386)
XLA Ops:
  7.2 2.0 fusion.104
  13.5 9.6 %all-gather.12 = bf16[1,1536]{1,0:T(2,128)(2,1)S(1)} all-gather(bf16[1,384]{1,0:T(2,128)(2,1)S(1)} %get-tuple-element.121), channel_id=14, replica_groups=mesh['shard'=4,'replica'=8] {'shard'}, dimensions={1}, use_global_device_ids=true | all-gather | bytes 3840 | tf_op jit(solution)/shard_map/all_gather | solution.py:186
  23.1 8.1 %all-gather.5 = bf16[1,1536]{1,0:T(2,128)(2,1)S(1)} all-gather(bf16[1,384]{1,0:T(2,128)(2,1)S(1)} %get-tuple-element.122), channel_id=7, replica_groups=mesh['shard'=4,'replica'=8] {'shard'}, dimensions={1}, use_global_device_ids=true | all-gather | bytes 3840 | tf_op jit(solution)/shard_map/all_gather | solution.py:186
  31.8 9.7 %all-gather = bf16[1,2,384]{1,0,2:T(2,128)(2,1)S(1)} all-gather(bf16[1,2,96]{1,0,2:T(2,128)(2,1)S(1)} %copy.131), channel_id=2, replica_groups=mesh['shard'=4,'replica'=8] {'shard'}, dimensions={2}, use_global_device_ids=true | all-gather | bytes 1920 | tf_op jit(solution)/shard_map/all_gather | solution.py:184
  41.7 1.7 slice_reduce_fusion.10
  43.4 8.5 %all-gather.1 = bf16[1,6,384]{1,0,2:T(2,128)(2,1)S(1)} all-gather(bf16[1,6,96]{1,0,2:T(2,128)(2,1)S(1)} %copy.132), channel_id=3, replica_groups=mesh['shard'=4,'replica'=8] {'shard'}, dimensions={2}, use_global_device_ids=true | all-gather | bytes 5760 | tf_op jit(solution)/shard_map/all_gather | solution.py:185
  52.1 8.3 %slice_reduce_fusion.8 = (f32[384]{0:T(512)S(1)}, f32[384]{0:T(512)S(1)}, f32[384]{0:T(512)S(1)}, f32[384]{0:T(512)S(1)}, f32[384]{0:T(512)S(1)}, /*index=5*/f32[384]{0:T(512)S(1)}) fusion(f32[1,6,384]{1,0,2:T(1,128)S(1)} %convert_element_type.258), kind=kLoop, calls=%fused_computation.158 | loop fusion | bytes 18432 | tf_op jit(solution)/shard_map/slice | solution.py:87
  60.4 10.1 %all-gather.7 = bf16[1,2,384]{1,0,2:T(2,128)(2,1)S(1)} all-gather(bf16[1,2,96]{1,0,2:T(2,128)(2,1)S(1)} %copy.133), channel_id=9, replica_groups=mesh['shard'=4,'replica'=8] {'shard'}, dimensions={2}, use_global_device_ids=true | all-gather | bytes 1920 | tf_op jit(solution)/shard_map/all_gather | solution.py:184
  70.7 1.7 slice_reduce_fusion.2
  72.5 8.6 %all-gather.8 = bf16[1,6,384]{1,0,2:T(2,128)(2,1)S(1)} all-gather(bf16[1,6,96]{1,0,2:T(2,128)(2,1)S(1)} %copy.134), channel_id=10, replica_groups=mesh['shard'=4,'replica'=8] {'shard'}, dimensions={2}, use_global_device_ids=true | all-gather | bytes 5760 | tf_op jit(solution)/shard_map/all_gather | solution.py:185
  81.2 8.3 %slice_reduce_fusion = (f32[384]{0:T(512)S(1)}, f32[384]{0:T(512)S(1)}, f32[384]{0:T(512)S(1)}, f32[384]{0:T(512)S(1)}, f32[384]{0:T(512)S(1)}, /*index=5*/f32[384]{0:T(512)S(1)}) fusion(f32[1,6,384]{1,0,2:T(1,128)S(1)} %convert_element_type.261), kind=kLoop, calls=%fused_computation.150 | loop fusion | bytes 18432 | tf_op jit(solution)/shard_map/slice | solution.py:87
  89.6 9.6 %all-gather.10 = bf16[1,384,384]{2,1,0:T(8,128)(2,1)S(1)} all-gather(bf16[1,96,384]{2,1,0:T(8,128)(2,1)S(1)} %get-tuple-element.117), channel_id=12, replica_groups=mesh['shard'=4,'replica'=8] {'shard'}, dimensions={1}, use_global_device_ids=true | all-gather | bytes 368640 | tf_op jit(solution)/shard_map/all_gather | solution.py:181
  99.2 11.1 %all-gather.3 = bf16[1,384,384]{2,1,0:T(8,128)(2,1)S(1)} all-gather(bf16[1,96,384]{2,1,0:T(8,128)(2,1)S(1)} %get-tuple-element.118), channel_id=5, replica_groups=mesh['shard'=4,'replica'=8] {'shard'}, dimensions={1}, use_global_device_ids=true | all-gather | bytes 368640 | tf_op jit(solution)/shard_map/all_gather | solution.py:181
  110.4 14.0 %all-gather.9 = bf16[1,384,1152]{2,1,0:T(8,128)(2,1)S(1)} all-gather(bf16[1,96,1152]{2,1,0:T(8,128)(2,1)S(1)} %get-tuple-element.107), channel_id=11, replica_groups=mesh['shard'=4,'replica'=8] {'shard'}, dimensions={1}, use_global_device_ids=true | all-gather | bytes 1105920 | tf_op jit(solution)/shard_map/all_gather | solution.py:180
  124.3 16.3 %all-gather.2 = bf16[1,384,1152]{2,1,0:T(8,128)(2,1)S(1)} all-gather(bf16[1,96,1152]{2,1,0:T(8,128)(2,1)S(1)} %get-tuple-element.108), channel_id=4, replica_groups=mesh['shard'=4,'replica'=8] {'shard'}, dimensions={1}, use_global_device_ids=true | all-gather | bytes 1105920 | tf_op jit(solution)/shard_map/all_gather | solution.py:180
  142.0 1.4 fusion.123
  143.4 2.2 convolution_convert_fusion.11
  146.3 2.9 multiply_convert_fusion.3
  149.2 1.8 fusion.115
  152.4 1.4 fusion.124
  153.8 2.2 convolution_convert_fusion.10
  156.6 3.1 multiply_convert_fusion.2
  159.8 2.6 fusion.121
  165.9 2.9 fusion.108
  168.7 1.4 fusion.125
  170.1 3.0 multiply_reduce_fusion.1
  173.1 1.5 multiply_convert_fusion.1
  175.8 2.3 multiply_reduce_fusion.3
  180.7 1.2 multiply_reduce_fusion.4
  184.7 1.5 convolution_convert_fusion.4
  186.3 2.9 fusion.106
  189.2 1.4 fusion.126
  190.6 1.7 multiply_reduce_fusion
  192.3 1.5 multiply_convert_fusion
  194.7 1.5 convolution_convert_fusion.5
  196.3 2.8 convolution_convert_fusion.2
  199.2 1.6 convolution_convert_fusion
  200.9 2.7 convolution_convert_fusion.3
  203.7 1.7 convolution_convert_fusion.1
  208.2 1.6 multiply_reduce_fusion.5
  211.8 9.1 %all-reduce.4 = (bf16[1536]{0:T(1024)(128)(2,1)S(1)}, bf16[1536]{0:T(1024)(128)(2,1)S(1)}) all-reduce(bf16[1536]{0:T(1024)(128)(2,1)S(1)} %get-tuple-element.147, bf16[1536]{0:T(1024)(128)(2,1)S(1)} %get-tuple-element.149), channel_id=29, replica_groups=mesh['shard'=4,'replica'=8] {'shard'}, use_global_device_ids=true, to_apply=%region_64.0.clone | all-reduce | flops 3072 | bytes 12288
  222.1 1.8 fusion.23
  223.9 1.6 bitcast_convert_fusion.7
  225.5 2.1 reduce-scatter.25.cloned.1.call-done
  227.6 1.6 bitcast_convert_fusion.8
  229.2 28.9 %reduce-scatter.23.cloned.1.call-done = bf16[96,1152]{1,0:T(8,128)(2,1)} async-done(((bf16[384,1152]{1,0:T(8,128)(2,1)}), bf16[96,1152]{1,0:T(8,128)(2,1)}) %reduce-scatter.23.cloned.1.call-update) | async-done | bytes 221200 | tf_op jit(solution)/shard_map/reduce_scatter | solution.py:204
  258.0 1.7 bitcast_convert_fusion.5
  259.8 28.1 %reduce-scatter.21.cloned.1.call-done = bf16[96,1152]{1,0:T(8,128)(2,1)} async-done(((bf16[384,1152]{1,0:T(8,128)(2,1)}), bf16[96,1152]{1,0:T(8,128)(2,1)}) %reduce-scatter.21.cloned.1.call-update) | async-done | bytes 221200 | tf_op jit(solution)/shard_map/reduce_scatter | solution.py:204
  287.9 1.7 bitcast_convert_fusion.6
  289.6 30.5 %reduce-scatter.31.cloned.1.call-done = bf16[96,1536]{1,0:T(8,128)(2,1)} async-done(((bf16[384,1536]{1,0:T(8,128)(2,1)}), bf16[96,1536]{1,0:T(8,128)(2,1)}) %reduce-scatter.31.cloned.1.call-update) | async-done | bytes 294928 | tf_op jit(solution)/shard_map/reduce_scatter | solution.py:210
  320.1 1.8 bitcast_convert_fusion.3
  321.9 29.7 %reduce-scatter.35.cloned.1.call-done = bf16[384,384]{1,0:T(8,128)(2,1)} async-done(((bf16[1536,384]{1,0:T(8,128)(2,1)}), bf16[384,384]{1,0:T(8,128)(2,1)}) %reduce-scatter.35.cloned.1.call-update) | async-done | bytes 294928 | tf_op jit(solution)/shard_map/reduce_scatter | solution.py:213
  351.6 1.8 bitcast_convert_fusion.1
  353.4 30.4 %reduce-scatter.29.cloned.1.call-done = bf16[96,1536]{1,0:T(8,128)(2,1)} async-done(((bf16[384,1536]{1,0:T(8,128)(2,1)}), bf16[96,1536]{1,0:T(8,128)(2,1)}) %reduce-scatter.29.cloned.1.call-update) | async-done | bytes 294928 | tf_op jit(solution)/shard_map/reduce_scatter | solution.py:210
  383.9 1.8 bitcast_convert_fusion.4
  385.7 29.7 %reduce-scatter.33.cloned.1.call-done = bf16[384,384]{1,0:T(8,128)(2,1)} async-done(((bf16[1536,384]{1,0:T(8,128)(2,1)}), bf16[384,384]{1,0:T(8,128)(2,1)}) %reduce-scatter.33.cloned.1.call-update) | async-done | bytes 294928 | tf_op jit(solution)/shard_map/reduce_scatter | solution.py:213
  415.4 1.8 bitcast_convert_fusion.2
  419.6 22.7 %reduce-scatter.39.cloned.1.call-done = bf16[96,2]{1,0:T(8,128)(2,1)} async-done(((bf16[384,2]{1,0:T(8,128)(2,1)}), bf16[96,2]{1,0:T(8,128)(2,1)}) %reduce-scatter.39.cloned.1.call-update) | async-done | bytes 400
  443.1 26.0 %reduce-scatter.37.cloned.1.call-done = bf16[96,2]{1,0:T(8,128)(2,1)} async-done(((bf16[384,2]{1,0:T(8,128)(2,1)}), bf16[96,2]{1,0:T(8,128)(2,1)}) %reduce-scatter.37.cloned.1.call-update) | async-done | bytes 400
  469.9 25.9 %reduce-scatter.43.cloned.1.call-done = bf16[96,6]{1,0:T(8,128)(2,1)} async-done(((bf16[384,6]{1,0:T(8,128)(2,1)}), bf16[96,6]{1,0:T(8,128)(2,1)}) %reduce-scatter.43.cloned.1.call-update) | async-done | bytes 1168
  496.6 26.0 %reduce-scatter.41.cloned.1.call-done = bf16[96,6]{1,0:T(8,128)(2,1)} async-done(((bf16[384,6]{1,0:T(8,128)(2,1)}), bf16[96,6]{1,0:T(8,128)(2,1)}) %reduce-scatter.41.cloned.1.call-update) | async-done | bytes 1168
  523.4 29.3 %all-reduce.2 = (f32[1,2,96]{2,1,0:T(2,128)S(1)}, f32[1,2,96]{2,1,0:T(2,128)S(1)}, f32[1,6,96]{2,1,0:T(8,128)S(1)}, f32[1,6,96]{2,1,0:T(8,128)S(1)}, f32[1,384]{1,0:T(1,128)S(1)}, /*index=5*/f32[1,384]{1,0:T(1,128)S(1)}) all-reduce(f32[1,2,96]{2,1,0:T(2,128)S(1)} %bitcast_convert_fusion.13, ...), channel_id=1, replica_groups=mesh['shard'=4,'replica'=8] {'replica'}, use_global_device_ids=true, to_apply=%region_43.0 | all-reduce | flops 2304 | bytes 18432 | tf_op jit(solution)/shard_map/psum | solution.py:226
  554.5 56.3 %all-reduce.7.cloned.1.call-done = (f32[1,96,1152]{2,1,0:T(8,128)}, f32[1,96,1152]{2,1,0:T(8,128)}, f32[1,96,384]{2,1,0:T(8,128)}, f32[1,96,384]{2,1,0:T(8,128)}...) async-done(((f32[1,96,1152]{2,1,0:T(8,128)}, f32[1,96,1152]{2,1,0:T(8,128)}, f32[1,96,384]{2,1,0:T(8,128)}, ...) | async-done | bytes 3538960 | tf_op jit(solution)/shard_map/psum | solution.py:226
  610.8 2.2 pad_maximum_fusion.2
  (258 shorter events, 36.1 us)
Async XLA Ops:
  7.2 2.1 copy-start.32
  7.2 139.1 %all-gather.19.cloned.1.call-start = ((), (), s32[]{:S(2)}) async-start(), calls=%async_computation.20 | async-start | bytes 1474560 | tf_op jit(solution)/shard_map/all_gather | solution.py:182
  9.2 3.0 copy-start
  9.2 4.3 copy-start.43
  9.2 4.3 copy-start.42
  9.2 22.0 %copy-start.41 = (bf16[2,6,96]{2,0,1:T(2,128)(2,1)S(1)}, bf16[2,6,96]{2,0,1:T(2,128)(2,1)}, u32[]{:S(2)}) copy-start(bf16[2,6,96]{2,0,1:T(2,128)(2,1)} %param.18) | copy-start | bytes 6916
  9.2 140.0 %all-gather.21.cloned.1.call-start = ((), (), s32[]{:S(2)}) async-start(), calls=%async_computation.21 | async-start | bytes 1474560 | tf_op jit(solution)/shard_map/all_gather | solution.py:183
  10.2 146.4 %all-gather.23.cloned.1.call-start = ((), (), s32[]{:S(2)}) async-start(), calls=%async_computation.22 | async-start | bytes 1474560 | tf_op jit(solution)/shard_map/all_gather | solution.py:182
  10.9 148.8 %all-gather.25.cloned.1.call-start = ((), (), s32[]{:S(2)}) async-start(), calls=%async_computation.23 | async-start | bytes 1474560 | tf_op jit(solution)/shard_map/all_gather | solution.py:183
  11.5 212.4 %reduce-scatter.27.cloned.1.call-start = ((), (), s32[]{:S(2)}) async-start(), calls=%async_computation.15 | async-start | bytes 368640 | tf_op jit(solution)/shard_map/reduce_scatter | solution.py:207
  70.5 19.1 %copy-start.38 = (bf16[2,96,384]{2,1,0:T(8,128)(2,1)S(1)}, bf16[2,96,384]{2,1,0:T(8,128)(2,1)}, u32[]{:S(2)}) copy-start(bf16[2,96,384]{2,1,0:T(8,128)(2,1)} %param.14) | copy-start | bytes 442372
  81.0 29.3 %copy-start.37 = (bf16[2,96,1152]{2,1,0:T(8,128)(2,1)S(1)}, bf16[2,96,1152]{2,1,0:T(8,128)(2,1)}, u32[]{:S(2)}) copy-start(bf16[2,96,1152]{2,1,0:T(8,128)(2,1)} %param.13) | copy-start | bytes 1327108
  110.3 35.4 %copy-start.18 = (bf16[1,384,384]{2,1,0:T(8,128)(2,1)}, bf16[1,384,384]{2,1,0:T(8,128)(2,1)S(1)}, u32[]{:S(2)}) copy-start(bf16[1,384,384]{2,1,0:T(8,128)(2,1)S(1)} %all-gather.3) | copy-start | bytes 884740
  124.3 27.0 %copy-start.12 = (bf16[1,384,1152]{2,1,0:T(8,128)(2,1)}, bf16[1,384,1152]{2,1,0:T(8,128)(2,1)S(1)}, u32[]{:S(2)}) copy-start(bf16[1,384,1152]{2,1,0:T(8,128)(2,1)S(1)} %all-gather.9) | copy-start | bytes 2654212
  141.7 3.9 copy-start.4
  141.9 3.8 copy-start.2
  142.0 3.6 copy-start.24
  152.0 3.9 copy-start.8
  152.2 3.8 copy-start.6
  152.3 3.6 copy-start.27
  156.6 3.1 copy-start.16
  159.8 2.6 copy-start.23
  162.3 1.2 copy-start.30
  173.1 1.5 copy-start.9
  173.1 1.9 copy-start.7
  174.6 1.2 copy-start.13
  175.3 52.3 %reduce-scatter.25.cloned.1.call-start = ((), (), s32[]{:S(2)}) async-start(), calls=%async_computation.14 | async-start | bytes 368640 | tf_op jit(solution)/shard_map/reduce_scatter | solution.py:207
  175.8 2.5 copy-start.21
  178.1 1.4 copy-start.20
  178.3 3.7 copy-start.14
  179.5 1.3 copy-start.22
  180.3 1.6 copy-start.31
  181.9 2.2 copy-start.19
  182.2 2.5 copy-start.51
  183.9 74.2 %reduce-scatter.23.cloned.1.call-start = ((), (), s32[]{:S(2)}) async-start(), calls=%async_computation.13 | async-start | bytes 1105920 | tf_op jit(solution)/shard_map/reduce_scatter | solution.py:204
  184.7 1.6 copy-start.28
  186.2 101.7 %reduce-scatter.21.cloned.1.call-start = ((), (), s32[]{:S(2)}) async-start(), calls=%async_computation.12 | async-start | bytes 1105920 | tf_op jit(solution)/shard_map/reduce_scatter | solution.py:204
  186.2 4.3 copy-start.3
  186.3 4.3 copy-start.5
  196.3 2.9 copy-start.1
  196.3 2.9 copy-start.17
  196.3 123.8 %reduce-scatter.31.cloned.1.call-start = ((), (), s32[]{:S(2)}) async-start(), calls=%async_computation.17 | async-start | bytes 1474560 | tf_op jit(solution)/shard_map/reduce_scatter | solution.py:210
  199.1 152.5 %reduce-scatter.35.cloned.1.call-start = ((), (), s32[]{:S(2)}) async-start(), calls=%async_computation.19 | async-start | bytes 1474560 | tf_op jit(solution)/shard_map/reduce_scatter | solution.py:213
  200.8 2.9 copy-start.15
  200.9 183.0 %reduce-scatter.29.cloned.1.call-start = ((), (), s32[]{:S(2)}) async-start(), calls=%async_computation.16 | async-start | bytes 1474560 | tf_op jit(solution)/shard_map/reduce_scatter | solution.py:210
  203.7 211.7 %reduce-scatter.33.cloned.1.call-start = ((), (), s32[]{:S(2)}) async-start(), calls=%async_computation.18 | async-start | bytes 1474560 | tf_op jit(solution)/shard_map/reduce_scatter | solution.py:213
  205.4 1.9 copy-start.47
  205.4 1.9 copy-start.48
  205.4 1.9 copy-start.49
  205.4 2.7 copy-start.11
  205.4 236.9 %reduce-scatter.39.cloned.1.call-start = ((), (), s32[]{:S(2)}) async-start(), calls=%async_computation.25 | async-start | bytes 122880
  208.2 2.6 copy-start.44
  208.2 2.8 copy-start.46
  208.2 12.9 %copy-start.45 = (bf16[384]{0:T(512)(128)(2,1)S(1)}, bf16[384]{0:T(512)(128)(2,1)}, u32[]{:S(2)}) copy-start(bf16[384]{0:T(512)(128)(2,1)} %get-tuple-element.57) | copy-start | bytes 2308
  209.8 259.3 %reduce-scatter.37.cloned.1.call-start = ((), (), s32[]{:S(2)}) async-start(), calls=%async_computation.24 | async-start | bytes 122880
  210.7 285.1 %reduce-scatter.43.cloned.1.call-start = ((), (), s32[]{:S(2)}) async-start(), calls=%async_computation.27 | async-start | bytes 122880
  220.9 301.7 %reduce-scatter.41.cloned.1.call-start = ((), (), s32[]{:S(2)}) async-start(), calls=%async_computation.26 | async-start | bytes 122880
  222.1 388.7 %all-reduce.7.cloned.1.call-start = ((), (), s32[]{:S(2)}) async-start(), calls=%async_computation.28 | async-start | bytes 7077888 | tf_op jit(solution)/shard_map/psum | solution.py:226
  610.8 2.2 copy-start.39
  610.8 2.2 copy-start.40
  610.8 3.0 copy-start.35
  610.8 3.0 copy-start.36
  613.8 1.2 copy-start.33
  613.8 1.7 copy-start.34
  (6 other events, 4.8 us)
Sparse Core Ops, SparseCore 0:
  10.4 31.4 all-gather.18
  44.3 29.3 all-gather.20
  76.1 30.4 all-gather.22
  108.9 32.1 all-gather.24
  175.4 24.5 reduce-scatter.26
  203.2 24.3 reduce-scatter.24
  231.1 26.8 reduce-scatter.22
  261.0 26.8 reduce-scatter.20
  291.4 28.6 reduce-scatter.30
  322.9 28.6 reduce-scatter.34
  355.1 28.6 reduce-scatter.28
  386.6 28.7 reduce-scatter.32
  418.1 24.1 reduce-scatter.38
  444.9 24.1 reduce-scatter.36
  471.7 24.1 reduce-scatter.42
  498.4 24.1 reduce-scatter.40
  526.0 84.7 all-reduce.6
where the time goes:
time: 632 us; the launch traced here: 623 us
  waiting for transfers between devices  338 us (53%)
  blocking collectives  144 us (23%)
  matrix products  57.1 us (9%)
  local copies, waits for them, and re-layouts  40.1 us (6%)
  other arithmetic  27 us (4%)
  between operations  16.6 us (3%)
    unnamed x21, waiting for transfers between devices  102 us
    reduce_scatter x2, waiting for transfers between devices, reduce_layer(): lax.psum_scatter(grads[2].astype(jnp.bfloat16), 'shard', scatter_dimensio...  60.9 us
    reduce_scatter x2, waiting for transfers between devices, reduce_layer(): lax.psum_scatter(grads[3].astype(jnp.bfloat16), 'shard', scatter_dimensio...  59.4 us
    reduce_scatter x2, waiting for transfers between devices, reduce_layer(): lax.psum_scatter(grads[0].astype(jnp.bfloat16), 'shard', scatter_dimensio...  57 us
    psum x1, waiting for transfers between devices, reduce_layer(): lax.psum((owned[0], owned[1], owned[2], owned[3], owned[4], owned[5], own...  56.3 us
    all_gather x2, blocking collectives, fetch_forward(): lax.all_gather(pieces[0], 'shard', axis=0, tiled=True)  30.3 us
    psum x1, blocking collectives, reduce_layer(): lax.psum((owned[0], owned[1], owned[2], owned[3], owned[4], owned[5], own...  29.3 us
    all_gather x2, blocking collectives, fetch_forward(): lax.all_gather(pieces[1], 'shard', axis=0, tiled=True)  20.7 us
  transfers between devices with their start and end apart: 17, of which 12 were waited for; matrix products, arithmetic and copies ran while one was open for 16% of the time, Pallas kernels for 0%

commit v1 on v0

--- a/solution.py
+++ b/solution.py
@@ -1,6 +1,10 @@
+import functools
+
 import jax
 import jax.numpy as jnp
 from jax import lax
+from jax.experimental import pallas as pl
+from jax.experimental.pallas import tpu as pltpu
 from jax.sharding import PartitionSpec as P
 
 D = 384
@@ -175,92 +179,318 @@
     return (stream_grad, grads)
 
 
-def fetch_forward(pieces):
-    return (
-        lax.all_gather(pieces[0], "shard", axis=0, tiled=True),
-        lax.all_gather(pieces[1], "shard", axis=0, tiled=True),
-        lax.all_gather(pieces[2], "shard", axis=0, tiled=True),
-        lax.all_gather(pieces[3], "shard", axis=0, tiled=True),
-        lax.all_gather(pieces[4], "shard", axis=1, tiled=True),
-        lax.all_gather(pieces[5], "shard", axis=1, tiled=True),
-        lax.all_gather(pieces[6], "shard", axis=0, tiled=True),
-    )
-
-
-def fetch_backward(pieces):
-    return (
-        lax.all_gather(pieces[0], "shard", axis=0, tiled=True),
-        lax.all_gather(pieces[1], "shard", axis=0, tiled=True),
-        lax.all_gather(pieces[2], "shard", axis=0, tiled=True),
-        lax.all_gather(pieces[3], "shard", axis=0, tiled=True),
-        lax.all_gather(pieces[4], "shard", axis=1, tiled=True),
-        lax.all_gather(pieces[5], "shard", axis=1, tiled=True),
-        lax.all_gather(pieces[6], "shard", axis=0, tiled=True),
-    )
-
-
-def reduce_layer(grads):
-    owned = (
-        lax.psum_scatter(
-            grads[0].astype(jnp.bfloat16), "shard", scatter_dimension=0, tiled=True
-        ).astype(jnp.float32),
-        lax.psum_scatter(
-            grads[1].astype(jnp.bfloat16), "shard", scatter_dimension=0, tiled=True
-        ).astype(jnp.float32),
-        lax.psum_scatter(
-            grads[2].astype(jnp.bfloat16), "shard", scatter_dimension=0, tiled=True
-        ).astype(jnp.float32),
-        lax.psum_scatter(
-            grads[3].astype(jnp.bfloat16), "shard", scatter_dimension=0, tiled=True
-        ).astype(jnp.float32),
-        lax.psum_scatter(
-            grads[4].astype(jnp.bfloat16), "shard", scatter_dimension=1, tiled=True
-        ).astype(jnp.float32),
-        lax.psum_scatter(
-            grads[5].astype(jnp.bfloat16), "shard", scatter_dimension=1, tiled=True
-        ).astype(jnp.float32),
-        lax.psum_scatter(
-            grads[6].astype(jnp.bfloat16), "shard", scatter_dimension=0, tiled=True
-        ).astype(jnp.float32),
-    )
-    return lax.psum(
-        (owned[0], owned[1], owned[2], owned[3], owned[4], owned[5], owned[6]), "replica"
-    )
-
-
-def on_device(images, cotangent, counts, w_qkv, w_out, w_up, w_down, gains, biases, up_bias):
-    stacks = (w_qkv, w_out, w_up, w_down, gains, biases, up_bias)
+MESH = pl.DeviceIdType.MESH
+
+
+def place(shards, replicas):
+    me = lax.axis_index("shard")
+    rep = lax.axis_index("replica")
+    core = lax.rem(rep, 2)
+    depth = lax.div(rep, 2)
+    return me, rep, core, depth, rep + 1 - 2 * core
+
+
+def gather_kernel(shards, layers, count, *refs):
+    ins = refs[: count + 1]
+    outs = refs[count + 1 : count + 2 + count * layers]
+    send, recv, psend, precv, ssend, srecv, local = refs[count + 2 + count * layers :]
+    me, rep, core, depth, mate = place(shards, 0)
+    barrier = pltpu.get_barrier_semaphore()
+    pl.semaphore_signal(barrier, inc=1, device_id=(me, mate), device_id_type=MESH)
+    for k in range(1, shards):
+        peer = lax.rem(me + k, shards)
+        pl.semaphore_signal(barrier, inc=1, device_id=(peer, rep), device_id_type=MESH)
+    pl.semaphore_wait(barrier, shards)
+    small_in, small_out = ins[count], outs[count * layers]
+    smalls = []
+    for k in range(1, shards):
+        peer = lax.rem(me + k, shards)
+        copy = pltpu.make_async_remote_copy(
+            src_ref=small_in, dst_ref=small_out.at[me], send_sem=ssend.at[k - 1],
+            recv_sem=srecv.at[k - 1], device_id=(peer, rep), device_id_type=MESH)
+        copy.start()
+        smalls.append(copy)
+    first = []
+    for layer in range(layers):
+        for a in range(count):
+            item = layer * count + a
+            for k in range(1, shards):
+                peer = lax.rem(me + k, shards)
+                copy = pltpu.make_async_remote_copy(
+                    src_ref=ins[a].at[layer, core], dst_ref=outs[item].at[me, core],
+                    send_sem=send.at[item, k - 1], recv_sem=recv.at[item, k - 1],
+                    device_id=(peer, rep), device_id_type=MESH)
+                copy.start()
+                first.append((item, k, copy))
+    own = []
+    for layer in range(layers):
+        for a in range(count):
+            item = layer * count + a
+            copy = pltpu.make_async_copy(ins[a].at[layer], outs[item].at[me], local.at[item])
+            copy.start()
+            own.append(copy)
+    copy = pltpu.make_async_copy(small_in, small_out.at[me], local.at[layers * count])
+    copy.start()
+    own.append(copy)
+    second = []
+    for item, k, copy in first:
+        origin = lax.rem(me + shards - k, shards)
+        copy.wait_recv()
+        piece = outs[item].at[origin, core]
+        passed = pltpu.make_async_remote_copy(
+            src_ref=piece, dst_ref=piece, send_sem=psend.at[item, k - 1],
+            recv_sem=precv.at[item, k - 1], device_id=(me, mate), device_id_type=MESH)
+        passed.start()
+        second.append(passed)
+    for copy in smalls:
+        copy.wait()
+    for copy in own:
+        copy.wait()
+    for item, k, copy in first:
+        copy.wait_send()
+    for copy in second:
+        copy.wait()
+
+
+def gather(stacks, shards):
+    weights = stacks[:4]
+    layers = weights[0].shape[0]
+    ins = [w.reshape(layers, 2, w.shape[1] // 2, w.shape[2]) for w in weights]
+    gains, biases, up_bias = stacks[4:]
+    width = gains.shape[2]
+    small = jnp.concatenate([gains, biases, up_bias.reshape(layers, -1, width)], 1)
+    rows = small.shape[1]
+    small = jnp.pad(small, ((0, 0), (0, -rows % 16), (0, -width % 128)))
+    count = len(ins)
+    shapes = [
+        jax.ShapeDtypeStruct((shards,) + w.shape[1:], w.dtype) for _ in range(layers) for w in ins
+    ]
+    shapes.append(jax.ShapeDtypeStruct((shards,) + small.shape, small.dtype))
+    sems = pltpu.SemaphoreType.DMA
+    items = layers * count
+    outs = pl.pallas_call(
+        functools.partial(gather_kernel, shards, layers, count),
+        out_shape=shapes,
+        in_specs=[pl.BlockSpec(memory_space=pltpu.VMEM)] * (count + 1),
+        out_specs=[pl.BlockSpec(memory_space=pl.ANY)] * len(shapes),
+        scratch_shapes=[
+            sems((items, shards - 1)), sems((items, shards - 1)),
+            sems((items, shards - 1)), sems((items, shards - 1)),
+            sems((shards - 1,)), sems((shards - 1,)), sems((items + 1,)),
+        ],
+        compiler_params=pltpu.CompilerParams(collective_id=0, has_side_effects=True),
+        name="gather_params",
+    )(*ins, small)
+    tiny = outs[-1][:, :, :rows, :width]
+    params = []
+    for layer in range(layers):
+        big = [outs[layer * count + a].reshape(-1, weights[a].shape[2]) for a in range(count)]
+        part = tiny[:, layer]
+        ng, nb = gains.shape[1], biases.shape[1]
+        params.append(tuple(big) + (
+            part[:, :ng].transpose(1, 0, 2).reshape(ng, -1),
+            part[:, ng : ng + nb].transpose(1, 0, 2).reshape(nb, -1),
+            part[:, ng + nb :].reshape(-1),
+        ))
+    return params
+
+
+def blocks_of(shape):
+    return [(r, c) for r in range(shape[0] // BLOCK) for c in range(shape[1] // 128)]
+
+
+def reduce_kernel(shards, deep, per, count, *refs):
+    ins, outs = refs[:count], refs[count : 2 * count]
+    refs = refs[2 * count :]
+    buf_a, buf_s, buf_b = refs[:count], refs[count : 2 * count], refs[2 * count : 3 * count]
+    z_own, z_recv, z_sum, z_all, z_mate = refs[3 * count : 3 * count + 5]
+    a_send, a_recv, b_send, b_recv, c_send, c_recv, d_send, d_recv, e_send, e_recv, loc = refs[
+        3 * count + 5 :
+    ]
+    me, rep, core, depth, mate = place(shards, deep)
+    barrier = pltpu.get_barrier_semaphore()
+    pl.semaphore_signal(barrier, inc=1, device_id=(me, mate), device_id_type=MESH)
+    for k in range(1, shards):
+        peer = lax.rem(me + k, shards)
+        pl.semaphore_signal(barrier, inc=1, device_id=(peer, rep), device_id_type=MESH)
+    for k in range(1, deep):
+        peer = lax.rem(depth + k, deep) * 2 + core
+        pl.semaphore_signal(barrier, inc=1, device_id=(me, peer), device_id_type=MESH)
+    pl.semaphore_wait(barrier, shards + deep - 1)
+
+    stage_a = []
+    for a in range(count):
+        copy = pltpu.make_async_remote_copy(
+            src_ref=ins[a].at[:, 1 - core], dst_ref=buf_a[a], send_sem=a_send.at[a],
+            recv_sem=a_recv.at[a], device_id=(me, mate), device_id_type=MESH)
+        copy.start()
+        stage_a.append(copy)
+    stage_b = []
+    for a in range(count):
+        stage_a[a].wait_recv()
+        for k in list(range(1, shards)) + [0]:
+            peer = lax.rem(me + k, shards)
+            mine = ins[a][peer, core].astype(jnp.float32)
+            buf_s[a][peer] = (mine + buf_a[a][peer].astype(jnp.float32)).astype(jnp.bfloat16)
+            if k:
+                copy = pltpu.make_async_remote_copy(
+                    src_ref=buf_s[a].at[peer], dst_ref=buf_b[a].at[k - 1],
+                    send_sem=b_send.at[a, k - 1], recv_sem=b_recv.at[a, k - 1],
+                    device_id=(peer, rep), device_id_type=MESH)
+                copy.start()
+                stage_b.append((a, copy))
+    number = 0
+    for a in range(count):
+        for owner, copy in stage_b:
+            if owner == a:
+                copy.wait_recv()
+        for r, c in blocks_of(buf_s[a].shape[1:]):
+            rows, cols = pl.ds(r * BLOCK, BLOCK), pl.ds(c * 128, 128)
+            total = buf_s[a][me, rows, cols].astype(jnp.float32)
+            for k in range(shards - 1):
+                total = total + buf_b[a][k, rows, cols].astype(jnp.float32)
+            z_own[number // per, number % per] = total.astype(jnp.bfloat16)
+            number += 1
+    while number < deep * per:
+        z_own[number // per, number % per] = jnp.zeros((BLOCK, 128), jnp.bfloat16)
+        number += 1
+    stage_c = []
+    for k in range(1, deep):
+        peer = lax.rem(depth + k, deep)
+        copy = pltpu.make_async_remote_copy(
+            src_ref=z_own.at[peer], dst_ref=z_recv.at[k - 1], send_sem=c_send.at[k - 1],
+            recv_sem=c_recv.at[k - 1], device_id=(me, peer * 2 + core), device_id_type=MESH)
+        copy.start()
+        stage_c.append(copy)
+    for copy in stage_c:
+        copy.wait_recv()
+    for b in range(per):
+        total = z_own[depth, b].astype(jnp.float32)
+        for k in range(deep - 1):
+            total = total + z_recv[k, b].astype(jnp.float32)
+        z_sum[b] = total.astype(jnp.bfloat16)
+    stage_d = []
+    for k in range(1, deep):
+        peer = lax.rem(depth + k, deep)
+        copy = pltpu.make_async_remote_copy(
+            src_ref=z_sum, dst_ref=z_all.at[depth], send_sem=d_send.at[k - 1],
+            recv_sem=d_recv.at[k - 1], device_id=(me, peer * 2 + core), device_id_type=MESH)
+        copy.start()
+        stage_d.append(copy)
+    own = pltpu.make_async_copy(z_sum, z_all.at[depth], loc.at[0])
+    own.start()
+    own.wait()
+    stage_e = []
+    for k in range(deep):
+        origin = lax.rem(depth + deep - k, deep)
+        if k:
+            stage_d[k - 1].wait_recv()
+        copy = pltpu.make_async_remote_copy(
+            src_ref=z_all.at[origin], dst_ref=z_mate.at[origin], send_sem=e_send.at[k],
+            recv_sem=e_recv.at[k], device_id=(me, mate), device_id_type=MESH)
+        copy.start()
+        stage_e.append(copy)
+
+    def put(held, half):
+        at = 0
+        for a in range(count):
+            for r, c in blocks_of(outs[a].shape[1:]):
+                rows, cols = pl.ds(r * BLOCK, BLOCK), pl.ds(c * 128, 128)
+                outs[a][half, rows, cols] = held[at // per, at % per].astype(jnp.float32)
+                at += 1
+
+    put(z_all, core)
+    for copy in stage_e:
+        copy.wait_recv()
+    put(z_mate, 1 - core)
+    for copy in stage_a + [c for _, c in stage_b] + stage_c + stage_d + stage_e:
+        copy.wait_send()
+
+
+BLOCK = 48
+
+
+def reduce_all(grads, shards, replicas):
+    layers = len(grads)
+    deep = replicas // 2
+    ins = []
+    for layer in range(layers):
+        for g in grads[layer][:4]:
+            ins.append(
+                g.astype(jnp.bfloat16).reshape(shards, 2, g.shape[0] // shards // 2, g.shape[1])
+            )
+    smalls = []
+    for layer in range(layers):
+        gg, gb, gu = grads[layer][4:]
+        width = gg.shape[1] // shards
+        smalls.append(jnp.concatenate([
+            gg.reshape(-1, shards, width).transpose(1, 0, 2),
+            gb.reshape(-1, shards, width).transpose(1, 0, 2),
+            gu.reshape(shards, -1, width),
+        ], 1))
+    ng, nb = grads[0][4].shape[0], grads[0][5].shape[0]
+    small = jnp.concatenate(smalls, 1)
+    rows = small.shape[1]
+    half = rows // 2
+    small = small.reshape(shards, 2, half, width).astype(jnp.bfloat16)
+    small = jnp.pad(small, ((0, 0), (0, 0), (0, -half % BLOCK), (0, -width % 128)))
+    ins.append(small)
+    count = len(ins)
+    shapes = [x.shape for x in ins]
+    total = sum(len(blocks_of(s[2:])) for s in shapes)
+    per = -(-total // deep)
+    sems = pltpu.SemaphoreType.DMA
+    vmem = lambda *s: pltpu.VMEM(s, jnp.bfloat16)
+    outs = pl.pallas_call(
+        functools.partial(reduce_kernel, shards, deep, per, count),
+        out_shape=[jax.ShapeDtypeStruct(s[1:], jnp.float32) for s in shapes],
+        in_specs=[pl.BlockSpec(memory_space=pltpu.VMEM)] * count,
+        out_specs=[pl.BlockSpec(memory_space=pltpu.VMEM)] * count,
+        scratch_shapes=[vmem(s[0], *s[2:]) for s in shapes]
+        + [vmem(s[0], *s[2:]) for s in shapes]
+        + [vmem(s[0] - 1, *s[2:]) for s in shapes]
+        + [
+            vmem(deep, per, BLOCK, 128), vmem(deep - 1, per, BLOCK, 128),
+            vmem(per, BLOCK, 128), vmem(deep, per, BLOCK, 128), vmem(deep, per, BLOCK, 128),
+            sems((count,)), sems((count,)),
+            sems((count, shards - 1)), sems((count, shards - 1)),
+            sems((deep - 1,)), sems((deep - 1,)),
+            sems((deep - 1,)), sems((deep - 1,)),
+            sems((deep,)), sems((deep,)), sems((1,)),
+        ],
+        compiler_params=pltpu.CompilerParams(
+            collective_id=1, has_side_effects=True, vmem_limit_bytes=56 * 1024 * 1024
+        ),
+        name="reduce_grads",
+    )(*ins)
+    big = [
+        jnp.stack([outs[layer * 4 + a].reshape(-1, shapes[a][3]) for layer in range(layers)], 0)
+        for a in range(4)
+    ]
+    tiny = outs[-1][:, :half, :width].reshape(layers, rows // layers, width)
+    return tuple(big) + (
+        tiny[:, :ng],
+        tiny[:, ng : ng + nb],
+        tiny[:, ng + nb :].reshape(layers, -1),
+    )
+
+
+def on_device(shards, replicas, images, cotangent, counts, *stacks):
     slot_count = images.shape[0]
     live = (jnp.arange(slot_count, dtype=jnp.int32) < counts[0]).astype(jnp.float32)[:, None, None]
-    held = []
+    params = gather(stacks, shards)
     kept = []
     stream = images
     for layer in range(LAYERS):
-        params = fetch_forward(tuple((stack[layer] for stack in stacks)))
-        held.append(params)
-        result, saved = forward_layer(stream, params)
+        stream, saved = forward_layer(stream, params[layer])
         kept.append(saved)
-        stream = result
     activations = stream * live
     grad = (cotangent * live).reshape(-1, D)
-    reduced = [None] * LAYERS
+    grads = [None] * LAYERS
     for layer in reversed(range(LAYERS)):
-        params = fetch_backward(tuple((stack[layer] for stack in stacks)))
-        grad, grads = backward_layer(kept[layer], grad, params)
-        reduced[layer] = reduce_layer(grads)
-    totals = tuple((jnp.stack([piece[index] for piece in reduced], 0) for index in range(7)))
-    input_grad = grad.reshape(images.shape)
-    return (
-        activations,
-        input_grad,
-        totals[0],
-        totals[1],
-        totals[2],
-        totals[3],
-        totals[4],
-        totals[5],
-        totals[6],
-    )
+        grad, grads[layer] = backward_layer(kept[layer], grad, params[layer])
+    totals = reduce_all(grads, shards, replicas)
+    return (activations, grad.reshape(images.shape)) + totals
 
 
 def solution(mesh):
@@ -288,5 +518,5 @@
         P(None, "shard"),
     )
     return jax.shard_map(
-        on_device, mesh=mesh, in_specs=in_specs, out_specs=out_specs, check_vma=False
-    )
+        functools.partial(on_device, mesh.shape["shard"], mesh.shape["replica"]), mesh=mesh, in_specs=in_specs, out_specs=out_specs, check_vma=False
+    )

time: 632 us -> 228 us (0.36)
  waiting for transfers between devices: 338 us -> 0 us
  blocking collectives: 144 us -> 0 us
  Pallas kernels: 0 us -> 138 us
  local copies, waits for them, and re-layouts: 40.1 us -> 22 us
  between operations: 16.6 us -> 1.93 us
  other arithmetic: 27 us -> 15.5 us
  matrix products: 57.1 us -> 47.2 us
    reduce_scatter x8 -> x0, waiting for transfers between devices: 179 us -> none  [the longest x2 60.9 us: reduce_layer(): lax.psum_scatter(grads[2].astype(jnp.bfloat16), 'shard', scatter_dimensio...]
    pallas_call x0 -> x2, Pallas kernels: none -> 138 us  [the longest x1 90.8 us: reduce_all(): pl.pallas_call(functools.partial(reduce_kernel, shards, deep, per, count)...]
    all_gather x10 -> x0, blocking collectives: 105 us -> none  [the longest x2 30.3 us: fetch_forward(): lax.all_gather(pieces[0], 'shard', axis=0, tiled=True)]
    unnamed x21 -> x0, waiting for transfers between devices: 102 us -> none
    psum x1 -> x0, waiting for transfers between devices: 56.3 us -> none  [reduce_layer(): lax.psum((owned[0], owned[1], owned[2], owned[3], owned[4], owned[5], own...]
    psum x1 -> x0, blocking collectives: 29.3 us -> none  [reduce_layer(): lax.psum((owned[0], owned[1], owned[2], owned[3], owned[4], owned[5], own...]
    slice x2, local copies, waits for them, and re-layouts: 16.7 us -> 0.12 us  [forward_layer(): result = middle + product(activated, w_down) + biases[5]]
    another operation x21 -> x4, other arithmetic: 20.2 us -> 5.14 us  [reduce_all(): jnp.stack([outs[layer * 4 + a].reshape(-1, shapes[a][3]) for layer in ran...]
  transfers between devices with their start and end apart: 17 -> 0, of which waited for: 12 -> 0; matrix products, arithmetic and copies ran while one was open for 16% -> 0% of each run, Pallas kernels for 0% -> 0%
where the time goes in v1:
time: 228 us; the launch traced here: 225 us
  Pallas kernels  138 us (61%)
  matrix products  47.2 us (21%)
  local copies, waits for them, and re-layouts  22 us (10%)
  other arithmetic  15.5 us (7%)
    pallas_call x1, Pallas kernels, reduce_all(): pl.pallas_call(functools.partial(reduce_kernel, shards, deep, per, count)...  90.8 us
    pallas_call x1, Pallas kernels, gather(): pl.pallas_call(functools.partial(gather_kernel, shards, layers, count), o...  47.3 us
    dot_general x8, matrix products, product_left(): lax.dot_general(left, right, (((0,), (0,)), ((), ())), preferred_element_...  16 us
    dot_general x12, matrix products, batched(): return jnp.einsum(form, left, right, preferred_element_type=jnp.float32)  13.6 us
    dot_general x8, matrix products, product_right(): lax.dot_general(left, right, (((1,), (1,)), ((), ())), preferred_element_...  9 us
    unnamed x103, local copies, waits for them, and re-layouts  8.13 us
    another operation x4, other arithmetic, reduce_all(): jnp.stack([outs[layer * 4 + a].reshape(-1, shapes[a][3]) for layer in ran...  5.14 us
    dot_general x8, matrix products, product(): return jnp.dot(left, right, preferred_element_type=jnp.float32)  4.97 us

profile of v1, /device:TPU:0, one launch (start us, length us, event | category | flops | bytes accessed | tf_op | source)
XLA Modules:
  0.0 224.7 jit_solution(2830656283694174882)
XLA Ops:
  1.3 1.0 fusion.45
  2.4 2.0 reduce_sum.342
  4.4 1.2 multiply_reduce_fusion.13
  5.6 0.8 reshape.506
  6.4 0.7 copy.70
  7.1 1.3 fusion.90.refs_4_
  8.4 47.3 %gather_params.1 = (bf16[4,2,48,1152]{3,2,1,0:T(8,128)(2,1)}, bf16[4,2,48,384]{3,2,1,0:T(8,128)(2,1)}, bf16[4,2,48,1536]{3,2,1,0:T(8,128)(2,1)}, bf16[4,2,192,38...) custom-call(bf16[2,2,48,1152]{3,2,1,0:T(8,128)(2,1)} %bitcast.245, ...), custom_call_target="tpu_custom_call" | custom-call | tf_op jit(solution)/shard_map/gather_params/pallas_call | solution.py:271
  55.7 0.8 slice_bitcast_fusion
  58.2 0.5 add_convert_fusion.4
  58.7 0.4 fusion.65
  60.1 0.5 convolution_convert_fusion.11
  60.6 0.5 copy-done.6
  61.8 0.7 copy-done.14
  62.4 1.6 multiply_convert_fusion.3
  64.1 0.6 fusion.109
  65.2 0.5 fusion.99
  66.3 1.4 fusion.118
  67.7 2.2 convolution_convert_fusion.10
  70.6 0.7 copy-done.16
  71.3 0.6 multiply_convert_fusion.2
  72.6 0.8 fusion.116
  73.5 0.5 fusion.23
  74.0 1.0 copy.91
  75.0 1.3 multiply_reduce_fusion.2
  76.4 0.7 stack.83
  77.0 1.2 fusion.101
  78.2 1.9 convolution_convert_fusion.13
  80.3 1.7 copy.80
  82.1 3.0 %fusion.104 = (bf16[6,64]{1,0:T(8,128)(2,1)S(1)}, bf16[1,197,6,64]{1,3,2,0:T(8,128)(2,1)}) fusion(bf16[197,6,64]{0,2,1:T(8,128)(2,1)} %bitcast.235, f32[6,197,197]{1,2,0:T(8,128)} %fusion.118), kind=kOutput, calls=%fused_computation.227 | convolution fusion | flops 30423310 | bytes 1234776 | tf_op jit(solution)/shard_map/bhqk,bqhe->bkhe/dot_general | solution.py:62
  85.1 1.9 convolution_convert_fusion.6
  87.0 2.7 %convolution_convert_fusion.1 = bf16[384,1536]{1,0:T(8,128)(2,1)} fusion(bf16[197,1536]{1,0:T(8,128)(2,1)} %copy-done.30, f32[197,384]{1,0:T(8,128)S(1)} %get-tuple-element.131, f32[384]{0:T(512)S(1)} %add.255, f32[384]{0:T(512)S(1)} %mul.339, f32[197]{0:T(256)S(1)} %add_rsqrt_fusion, f32[197]{0:T(256)S(1)} %broadcast_multiply_fusion.8), kind=kOutput, calls=%fused_computation.3 | convolution fusion | flops 233358720 | bytes 2092072 | tf_op jit(solution)/shard_map/dot_general | solution.py:50
  89.8 1.8 convolution_convert_fusion
  92.0 3.0 %multiply_reduce_fusion.1 = (f32[6,197]{1,0:T(8,128)S(1)}, f32[6,197,197]{1,2,0:T(8,128)}) fusion(f32[6,197,197]{1,2,0:T(8,128)S(1)} %fusion.119, bf16[197,6,64]{0,2,1:T(8,128)(2,1)} %bitcast.201, bf16[197,6,64]{0,2,1:T(8,128)(2,1)} %bitcast.198), kind=kOutput, calls=%fused_computation.31 | convolution fusion | flops 60309384 | bytes 2170152 | tf_op jit(solution)/shard_map/reduce_sum | solution.py:82
  94.9 1.6 multiply_convert_fusion.1
  96.5 1.0 convolution_convert_fusion.9
  97.6 0.9 fusion.105
  98.6 2.4 %multiply_reduce_fusion.3 = (bf16[384]{0:T(512)(128)(2,1)S(1)}, f32[197]{0:T(256)S(1)}, f32[197]{0:T(256)S(1)}, bf16[384]{0:T(512)(128)(2,1)}, f32[197,384]{1,0:T(8,128)S(1)}) fusion(f32[197,384]{1,0:T(8,128)S(1)} %get-tuple-element.129, f32[197]{0:T(256)S(1)} %add_rsqrt_fusion.1, f32[197]{0:T(256)S(1)} %broadcast_multiply_fusion.9, f32[384]{0:T(512)S(1)} %mul.332, ...), kind=kOutput, calls=%fused_computation.86 | convolution fusion | flops 176334336 | bytes 1950032 | tf_op jit(solution)/shard_map/dot_general | solution.py:56
  100.9 0.7 stack.82
  101.8 2.7 %convolution_convert_fusion.2 = bf16[384,1152]{1,0:T(8,128)(2,1)} fusion(bf16[197,384]{0,1:T(8,128)(2,1)} %bitcast.263, bf16[197,384]{0,1:T(8,128)(2,1)} %bitcast.253, bf16[197,384]{0,1:T(8,128)(2,1)} %bitcast.255, f32[197,384]{1,0:T(8,128)S(1)} %get-tuple-element.129, f32[384]{0:T(512)S(1)} %add.241, f32[384]{0:T(512)S(1)} %mul.332, ...), kind=kOutput, calls=%fused_computation.4 | convolution fusion | flops 176475264 | bytes 1645864 | tf_op jit(solution)/shard_map/dot_general | solution.py:50
  104.6 0.8 fusion.115
  105.8 0.7 multiply_reduce_fusion.4
  106.7 0.6 stack.73
  108.0 0.6 stack.78
  109.0 2.9 %fusion.106 = (bf16[6,64]{1,0:T(8,128)(2,1)S(1)}, bf16[1,197,6,64]{1,3,2,0:T(8,128)(2,1)}) fusion(bf16[197,6,64]{0,2,1:T(8,128)(2,1)S(1)} %bitcast.237, f32[6,197,197]{1,2,0:T(8,128)} %copy-done.6), kind=kOutput, calls=%fused_computation.229 | convolution fusion | flops 30423310 | bytes 1234776 | tf_op jit(solution)/shard_map/bhqk,bqhe->bkhe/dot_general | solution.py:62
  111.9 1.0 convolution_convert_fusion.7
  112.9 2.7 %convolution_convert_fusion.4 = bf16[384,1536]{1,0:T(8,128)(2,1)} fusion(bf16[197,1536]{1,0:T(8,128)(2,1)} %copy-done.29, f32[197,384]{1,0:T(8,128)S(1)} %get-tuple-element.125, f32[384]{0:T(512)S(1)} %add.230, f32[384]{0:T(512)S(1)} %mul.323, f32[197]{0:T(256)S(1)} %add_rsqrt_fusion.2, f32[197]{0:T(256)S(1)} %broadcast_multiply_fusion.10), kind=kOutput, calls=%fused_computation.6 | convolution fusion | flops 233358720 | bytes 2092072 | tf_op jit(solution)/shard_map/dot_general | solution.py:50
  115.6 1.6 convolution_convert_fusion.3
  117.6 0.7 multiply_reduce_fusion
  119.3 0.4 copy-done.18
  119.7 0.7 multiply_reduce_fusion.5
  120.8 1.0 copy.92
  122.1 0.7 pad.9.refs_8_
  122.7 1.5 convolution_convert_fusion.5
  124.2 90.8 %reduce_grads.1 = (f32[2,48,1152]{2,1,0:T(8,128)}, f32[2,48,384]{2,1,0:T(8,128)}, f32[2,48,1536]{2,1,0:T(8,128)}, f32[2,192,384]{2,1,0:T(8,128)}, f32[2,48,1152]...) custom-call(bf16[4,2,48,1152]{3,2,1,0:T(8,128)(2,1)} %bitcast.226, ...), custom_call_target="tpu_custom_call" | custom-call | tf_op jit(solution)/shard_map/reduce_grads/pallas_call | solution.py:444
  215.1 2.2 pad_maximum_fusion.2
  217.3 1.3 slice.158
  218.6 0.7 slice.160
  219.3 0.7 slice.159
  220.0 0.6 copy.93
  220.6 0.7 reshape.541
  221.2 0.7 pad_maximum_fusion.5
  222.0 1.1 pad_maximum_fusion
  223.2 0.4 copy-done.32
  223.7 1.1 pad_maximum_fusion.1
  (181 shorter events, 10.5 us)
Async XLA Ops:
  4.4 53.8 %copy-start = (f32[1,197,384]{2,0,1:T(1,128)S(1)}, f32[1,197,384]{2,0,1:T(1,128)}, u32[]{:S(2)}) copy-start(f32[1,197,384]{2,0,1:T(1,128)} %param.10) | copy-start | bytes 907780
  55.7 3.0 %copy-start.17 = (bf16[4,2,48,1152]{3,2,1,0:T(8,128)(2,1)S(1)}, bf16[4,2,48,1152]{3,2,1,0:T(8,128)(2,1)}, u32[]{:S(2)}) copy-start(bf16[4,2,48,1152]{3,2,1,0:T(8,128)(2,1)} %get-tuple-element.28) | copy-start | bytes 2654212
  59.7 0.9 copy-start.21
  59.7 1.4 copy-start.11
  60.0 1.0 copy-start.6
  61.1 0.7 copy-start.23
  61.1 1.3 copy-start.14
  62.4 1.6 copy-start.8
  64.1 1.2 copy-start.19
  65.9 3.9 %copy-start.3 = (bf16[197,384]{0,1:T(8,128)(2,1)}, bf16[197,384]{0,1:T(8,128)(2,1)S(1)}, u32[]{:S(2)}) copy-start(bf16[197,384]{0,1:T(8,128)(2,1)S(1)} %copy.76) | copy-start | bytes 453892
  66.1 3.8 %copy-start.1 = (bf16[197,384]{0,1:T(8,128)(2,1)}, bf16[197,384]{0,1:T(8,128)(2,1)S(1)}, u32[]{:S(2)}) copy-start(bf16[197,384]{0,1:T(8,128)(2,1)S(1)} %copy.77) | copy-start | bytes 453892
  66.3 3.6 %copy-start.25 = (bf16[197,384]{0,1:T(8,128)(2,1)}, bf16[197,384]{0,1:T(8,128)(2,1)S(1)}, u32[]{:S(2)}) copy-start(bf16[197,384]{0,1:T(8,128)(2,1)S(1)} %copy.75) | copy-start | bytes 453892
  66.3 3.7 %copy-start.13 = (bf16[4,2,48,384]{3,2,1,0:T(8,128)(2,1)S(1)}, bf16[4,2,48,384]{3,2,1,0:T(8,128)(2,1)}, u32[]{:S(2)}) copy-start(bf16[4,2,48,384]{3,2,1,0:T(8,128)(2,1)} %get-tuple-element.33) | copy-start | bytes 884740
  69.9 0.7 copy-start.27
  69.9 1.3 copy-start.16
  71.3 1.0 copy-start.5
  71.3 1.4 copy-start.10
  73.5 1.5 copy-start.30
  89.8 1.8 copy-start.26
  89.8 1.8 copy-start.28
  94.9 1.6 copy-start.4
  94.9 2.6 %copy-start.2 = (bf16[197,384]{0,1:T(8,128)(2,1)S(1)}, bf16[197,384]{0,1:T(8,128)(2,1)}, u32[]{:S(2)}) copy-start(bf16[197,384]{0,1:T(8,128)(2,1)} %copy-done.1) | copy-start | bytes 453892
  96.5 2.0 copy-start.20
  101.6 3.0 %copy-start.9 = (bf16[4,2,192,384]{3,2,1,0:T(8,128)(2,1)S(1)}, bf16[4,2,192,384]{3,2,1,0:T(8,128)(2,1)}, u32[]{:S(2)}) copy-start(bf16[4,2,192,384]{3,2,1,0:T(8,128)(2,1)} %get-tuple-element.31) | copy-start | bytes 3538948
  101.8 2.8 %copy-start.7 = (f32[197,1536]{1,0:T(8,128)S(1)}, f32[197,1536]{1,0:T(8,128)}, u32[]{:S(2)}) copy-start(f32[197,1536]{1,0:T(8,128)} %get-tuple-element.127) | copy-start | bytes 3631108
  104.6 1.3 copy-start.15
  105.4 1.1 copy-start.29
  106.6 1.1 copy-start.12
  106.6 2.1 copy-start.41
  107.6 4.3 %copy-start.24 = (bf16[6,64,197]{2,1,0:T(8,128)(2,1)S(1)}, bf16[6,64,197]{2,1,0:T(8,128)(2,1)}, u32[]{:S(2)}) copy-start(bf16[6,64,197]{2,1,0:T(8,128)(2,1)} %copy-done.23) | copy-start | bytes 453892
  115.6 1.6 copy-start.22
  118.5 1.2 copy-start.18
  118.5 1.2 copy-start.42
  120.4 1.5 copy-start.37
  120.4 1.5 copy-start.40
  120.4 1.5 copy-start.38
  120.5 1.5 copy-start.39
  215.0 6.2 %copy-start.35 = (f32[2,48,384]{2,1,0:T(8,128)S(1)}, f32[2,48,384]{2,1,0:T(8,128)}, u32[]{:S(2)}) copy-start(f32[2,48,384]{2,1,0:T(8,128)} %get-tuple-element.38) | copy-start | bytes 442372
  215.1 6.2 %copy-start.36 = (f32[2,48,384]{2,1,0:T(8,128)S(1)}, f32[2,48,384]{2,1,0:T(8,128)}, u32[]{:S(2)}) copy-start(f32[2,48,384]{2,1,0:T(8,128)} %get-tuple-element.39) | copy-start | bytes 442372
  215.1 6.9 %copy-start.33 = (f32[2,48,1536]{2,1,0:T(8,128)S(1)}, f32[2,48,1536]{2,1,0:T(8,128)}, u32[]{:S(2)}) copy-start(f32[2,48,1536]{2,1,0:T(8,128)} %get-tuple-element.40) | copy-start | bytes 1769476
  215.1 6.9 %copy-start.34 = (f32[2,48,1536]{2,1,0:T(8,128)S(1)}, f32[2,48,1536]{2,1,0:T(8,128)}, u32[]{:S(2)}) copy-start(f32[2,48,1536]{2,1,0:T(8,128)} %get-tuple-element.41) | copy-start | bytes 1769476
  222.0 1.3 copy-start.31
  222.0 1.7 copy-start.32

commit v2 on v1

--- a/solution.py
+++ b/solution.py
@@ -210,18 +210,19 @@
             recv_sem=srecv.at[k - 1], device_id=(peer, rep), device_id_type=MESH)
         copy.start()
         smalls.append(copy)
+    side = (me + 1 - 2 * lax.rem(me, 2), lax.rem(me + 2, shards))
+    items = layers * count
     first = []
     for layer in range(layers):
         for a in range(count):
             item = layer * count + a
-            for k in range(1, shards):
-                peer = lax.rem(me + k, shards)
+            for k in range(2):
                 copy = pltpu.make_async_remote_copy(
                     src_ref=ins[a].at[layer, core], dst_ref=outs[item].at[me, core],
-                    send_sem=send.at[item, k - 1], recv_sem=recv.at[item, k - 1],
-                    device_id=(peer, rep), device_id_type=MESH)
+                    send_sem=send.at[item, k], recv_sem=recv.at[item, k],
+                    device_id=(side[k], rep), device_id_type=MESH)
                 copy.start()
-                first.append((item, k, copy))
+                first.append(copy)
     own = []
     for layer in range(layers):
         for a in range(count):
@@ -233,20 +234,37 @@
     copy.start()
     own.append(copy)
     second = []
-    for item, k, copy in first:
-        origin = lax.rem(me + shards - k, shards)
-        copy.wait_recv()
+
+    def to_mate(item, slot, origin):
         piece = outs[item].at[origin, core]
         passed = pltpu.make_async_remote_copy(
-            src_ref=piece, dst_ref=piece, send_sem=psend.at[item, k - 1],
-            recv_sem=precv.at[item, k - 1], device_id=(me, mate), device_id_type=MESH)
+            src_ref=piece, dst_ref=piece, send_sem=psend.at[item, slot],
+            recv_sem=precv.at[item, slot], device_id=(me, mate), device_id_type=MESH)
         passed.start()
         second.append(passed)
+
+    relays = [None] * items
+    for item in range(items + 1):
+        if item < items:
+            via = (item + item // count) % 2
+            for k in (via, 1 - via):
+                first[2 * item + k].wait_recv()
+                if k == via:
+                    piece = outs[item].at[side[via], core]
+                    relays[item] = pltpu.make_async_remote_copy(
+                        src_ref=piece, dst_ref=piece, send_sem=send.at[item, 2],
+                        recv_sem=recv.at[item, 2], device_id=(side[1 - via], rep),
+                        device_id_type=MESH)
+                    relays[item].start()
+                to_mate(item, k, side[k])
+        if item > 0:
+            relays[item - 1].wait_recv()
+            to_mate(item - 1, 2, shards - 1 - me)
     for copy in smalls:
         copy.wait()
     for copy in own:
         copy.wait()
-    for item, k, copy in first:
+    for copy in first + relays:
         copy.wait_send()
     for copy in second:
         copy.wait()
@@ -295,130 +313,166 @@
     return params
 
 
+BLOCK = 48
+
+
 def blocks_of(shape):
     return [(r, c) for r in range(shape[0] // BLOCK) for c in range(shape[1] // 128)]
 
 
-def reduce_kernel(shards, deep, per, count, *refs):
-    ins, outs = refs[:count], refs[count : 2 * count]
-    refs = refs[2 * count :]
+def reduce_kernel(shards, deep, plan, groups, pers, turn, *refs):
+    count = len(plan)
+    kinds = 1 + max(kind for kind, _, _ in plan)
+    many = len(groups)
+    ins, outs = refs[:count], refs[count : count + kinds]
+    refs = refs[count + kinds :]
     buf_a, buf_s, buf_b = refs[:count], refs[count : 2 * count], refs[2 * count : 3 * count]
-    z_own, z_recv, z_sum, z_all, z_mate = refs[3 * count : 3 * count + 5]
+    z_own, z_recv, z_sum, z_all, z_mate = [
+        refs[3 * count + n * many : 3 * count + (n + 1) * many] for n in range(5)
+    ]
     a_send, a_recv, b_send, b_recv, c_send, c_recv, d_send, d_recv, e_send, e_recv, loc = refs[
-        3 * count + 5 :
+        3 * count + 5 * many :
     ]
     me, rep, core, depth, mate = place(shards, deep)
+    side = (me + 1 - 2 * lax.rem(me, 2), lax.rem(me + 2, shards))
+    far = shards - 1 - me
     barrier = pltpu.get_barrier_semaphore()
     pl.semaphore_signal(barrier, inc=1, device_id=(me, mate), device_id_type=MESH)
-    for k in range(1, shards):
-        peer = lax.rem(me + k, shards)
-        pl.semaphore_signal(barrier, inc=1, device_id=(peer, rep), device_id_type=MESH)
+    for k in range(2):
+        pl.semaphore_signal(barrier, inc=1, device_id=(side[k], rep), device_id_type=MESH)
     for k in range(1, deep):
         peer = lax.rem(depth + k, deep) * 2 + core
         pl.semaphore_signal(barrier, inc=1, device_id=(me, peer), device_id_type=MESH)
-    pl.semaphore_wait(barrier, shards + deep - 1)
-
-    stage_a = []
-    for a in range(count):
+    pl.semaphore_wait(barrier, deep + 2)
+
+    def wide(value):
+        return value.astype(jnp.float32)
+
+    def remote(src, dst, send, recv, device):
         copy = pltpu.make_async_remote_copy(
-            src_ref=ins[a].at[:, 1 - core], dst_ref=buf_a[a], send_sem=a_send.at[a],
-            recv_sem=a_recv.at[a], device_id=(me, mate), device_id_type=MESH)
+            src_ref=src, dst_ref=dst, send_sem=send, recv_sem=recv, device_id=device,
+            device_id_type=MESH)
         copy.start()
-        stage_a.append(copy)
-    stage_b = []
-    for a in range(count):
-        stage_a[a].wait_recv()
-        for k in list(range(1, shards)) + [0]:
-            peer = lax.rem(me + k, shards)
-            mine = ins[a][peer, core].astype(jnp.float32)
-            buf_s[a][peer] = (mine + buf_a[a][peer].astype(jnp.float32)).astype(jnp.bfloat16)
-            if k:
-                copy = pltpu.make_async_remote_copy(
-                    src_ref=buf_s[a].at[peer], dst_ref=buf_b[a].at[k - 1],
-                    send_sem=b_send.at[a, k - 1], recv_sem=b_recv.at[a, k - 1],
-                    device_id=(peer, rep), device_id_type=MESH)
-                copy.start()
-                stage_b.append((a, copy))
-    number = 0
-    for a in range(count):
-        for owner, copy in stage_b:
-            if owner == a:
-                copy.wait_recv()
-        for r, c in blocks_of(buf_s[a].shape[1:]):
-            rows, cols = pl.ds(r * BLOCK, BLOCK), pl.ds(c * 128, 128)
-            total = buf_s[a][me, rows, cols].astype(jnp.float32)
-            for k in range(shards - 1):
-                total = total + buf_b[a][k, rows, cols].astype(jnp.float32)
-            z_own[number // per, number % per] = total.astype(jnp.bfloat16)
+        return copy
+
+    stage_a = {}
+    for group in groups:
+        for a in group:
+            stage_a[a] = remote(
+                ins[a].at[:, 1 - core], buf_a[a], a_send.at[a], a_recv.at[a], (me, mate))
+    one, two, stage_c, stage_d, stage_e = {}, {}, {}, {}, {}
+
+    def pair(a, dest):
+        return wide(ins[a][dest, core]) + wide(buf_a[a][dest])
+
+    def do_one(g):
+        for a in groups[g]:
+            stage_a[a].wait_recv()
+            near = side[turn[a]]
+            buf_s[a][0] = pair(a, near).astype(jnp.bfloat16)
+            buf_s[a][1] = pair(a, far).astype(jnp.bfloat16)
+            one[a] = remote(
+                buf_s[a].at[pl.ds(0, 2)], buf_b[a].at[pl.ds(0, 2)], b_send.at[a, 0],
+                b_recv.at[a, 0], (near, rep))
+
+    def do_two(g):
+        for a in groups[g]:
+            one[a].wait_recv()
+            near = side[1 - turn[a]]
+            buf_s[a][2] = (pair(a, near) + wide(buf_b[a][1])).astype(jnp.bfloat16)
+            two[a] = remote(
+                buf_s[a].at[2], buf_b[a].at[2], b_send.at[a, 1], b_recv.at[a, 1], (near, rep))
+
+    def do_scatter(g):
+        per, number = pers[g], 0
+        for a in groups[g]:
+            two[a].wait_recv()
+            for r, c in blocks_of(buf_a[a].shape[1:]):
+                rows, cols = pl.ds(r * BLOCK, BLOCK), pl.ds(c * 128, 128)
+                total = wide(ins[a][me, core, rows, cols]) + wide(buf_a[a][me, rows, cols])
+                total = total + wide(buf_b[a][0, rows, cols]) + wide(buf_b[a][2, rows, cols])
+                z_own[g][number // per, number % per] = total.astype(jnp.bfloat16)
+                number += 1
+        while number < deep * per:
+            z_own[g][number // per, number % per] = jnp.zeros((BLOCK, 128), jnp.bfloat16)
             number += 1
-    while number < deep * per:
-        z_own[number // per, number % per] = jnp.zeros((BLOCK, 128), jnp.bfloat16)
-        number += 1
-    stage_c = []
-    for k in range(1, deep):
-        peer = lax.rem(depth + k, deep)
-        copy = pltpu.make_async_remote_copy(
-            src_ref=z_own.at[peer], dst_ref=z_recv.at[k - 1], send_sem=c_send.at[k - 1],
-            recv_sem=c_recv.at[k - 1], device_id=(me, peer * 2 + core), device_id_type=MESH)
-        copy.start()
-        stage_c.append(copy)
-    for copy in stage_c:
-        copy.wait_recv()
-    for b in range(per):
-        total = z_own[depth, b].astype(jnp.float32)
-        for k in range(deep - 1):
-            total = total + z_recv[k, b].astype(jnp.float32)
-        z_sum[b] = total.astype(jnp.bfloat16)
-    stage_d = []
-    for k in range(1, deep):
-        peer = lax.rem(depth + k, deep)
-        copy = pltpu.make_async_remote_copy(
-            src_ref=z_sum, dst_ref=z_all.at[depth], send_sem=d_send.at[k - 1],
-            recv_sem=d_recv.at[k - 1], device_id=(me, peer * 2 + core), device_id_type=MESH)
-        copy.start()
-        stage_d.append(copy)
-    own = pltpu.make_async_copy(z_sum, z_all.at[depth], loc.at[0])
-    own.start()
-    own.wait()
-    stage_e = []
-    for k in range(deep):
-        origin = lax.rem(depth + deep - k, deep)
-        if k:
-            stage_d[k - 1].wait_recv()
-        copy = pltpu.make_async_remote_copy(
-            src_ref=z_all.at[origin], dst_ref=z_mate.at[origin], send_sem=e_send.at[k],
-            recv_sem=e_recv.at[k], device_id=(me, mate), device_id_type=MESH)
-        copy.start()
-        stage_e.append(copy)
-
-    def put(held, half):
-        at = 0
-        for a in range(count):
-            for r, c in blocks_of(outs[a].shape[1:]):
-                rows, cols = pl.ds(r * BLOCK, BLOCK), pl.ds(c * 128, 128)
-                outs[a][half, rows, cols] = held[at // per, at % per].astype(jnp.float32)
+        stage_c[g] = []
+        for k in range(1, deep):
+            peer = lax.rem(depth + k, deep)
+            stage_c[g].append(remote(
+                z_own[g].at[peer], z_recv[g].at[k - 1], c_send.at[g, k - 1],
+                c_recv.at[g, k - 1], (me, peer * 2 + core)))
+
+    def do_spread(g):
+        for copy in stage_c[g]:
+            copy.wait_recv()
+        for b in range(pers[g]):
+            total = wide(z_own[g][depth, b])
+            for k in range(deep - 1):
+                total = total + wide(z_recv[g][k, b])
+            z_sum[g][b] = total.astype(jnp.bfloat16)
+        stage_d[g] = []
+        for k in range(1, deep):
+            peer = lax.rem(depth + k, deep)
+            stage_d[g].append(remote(
+                z_sum[g], z_all[g].at[depth], d_send.at[g, k - 1], d_recv.at[g, k - 1],
+                (me, peer * 2 + core)))
+        own = pltpu.make_async_copy(z_sum[g], z_all[g].at[depth], loc.at[g])
+        own.start()
+        own.wait()
+
+    def do_swap(g):
+        for copy in stage_d[g]:
+            copy.wait_recv()
+        stage_e[g] = remote(z_all[g], z_mate[g], e_send.at[g], e_recv.at[g], (me, mate))
+        put(g, z_all[g], core)
+
+    def do_last(g):
+        stage_e[g].wait_recv()
+        put(g, z_mate[g], 1 - core)
+
+    def put(g, held, half):
+        per, at = pers[g], 0
+        for a in groups[g]:
+            kind, layer, start = plan[a]
+            for r, c in blocks_of(buf_a[a].shape[1:]):
+                rows, cols = pl.ds(r * BLOCK, BLOCK), pl.ds(start + c * 128, 128)
+                outs[kind][layer, half, rows, cols] = wide(held[at // per, at % per])
                 at += 1
 
-    put(z_all, core)
-    for copy in stage_e:
-        copy.wait_recv()
-    put(z_mate, 1 - core)
-    for copy in stage_a + [c for _, c in stage_b] + stage_c + stage_d + stage_e:
-        copy.wait_send()
-
-
-BLOCK = 48
+    stages = (do_one, do_two, do_scatter, do_spread, do_swap, do_last)
+    for t in range(many + len(stages) - 1):
+        for n, stage in enumerate(stages):
+            if 0 <= t - n < many:
+                stage(t - n)
+    for group in (stage_a, one, two, stage_e):
+        for copy in group.values():
+            copy.wait_send()
+    for group in (stage_c, stage_d):
+        for copies in group.values():
+            for copy in copies:
+                copy.wait_send()
 
 
 def reduce_all(grads, shards, replicas):
     layers = len(grads)
     deep = replicas // 2
-    ins = []
-    for layer in range(layers):
-        for g in grads[layer][:4]:
-            ins.append(
-                g.astype(jnp.bfloat16).reshape(shards, 2, g.shape[0] // shards // 2, g.shape[1])
-            )
+    ins, plan, groups = [], [], []
+    for layer in reversed(range(layers)):
+        qkv, out, up, down = grads[layer][:4]
+        cut = (qkv.shape[1] + out.shape[1]) // 2
+        order = [[(3, down, 0), (2, up, 0)], [(0, qkv[:, :cut], 0), (0, qkv[:, cut:], cut), (1, out, 0)]]
+        for part in order:
+            group = []
+            for kind, g, start in part:
+                group.append(len(ins))
+                plan.append((kind, layer, start))
+                ins.append(
+                    g.astype(jnp.bfloat16).reshape(shards, 2, g.shape[0] // shards // 2, g.shape[1])
+                )
+            if len(group) == 3:
+                group = [group[0], group[1], None, group[2]]
+            groups.append(group)
     smalls = []
     for layer in range(layers):
         gg, gb, gu = grads[layer][4:]
@@ -434,40 +488,51 @@
     half = rows // 2
     small = small.reshape(shards, 2, half, width).astype(jnp.bfloat16)
     small = jnp.pad(small, ((0, 0), (0, 0), (0, -half % BLOCK), (0, -width % 128)))
+    groups[-1].append(len(ins))
+    plan.append((4, 0, 0))
     ins.append(small)
     count = len(ins)
+    turns = [None] * count
+    for group in groups:
+        for n, a in enumerate(group):
+            if a is not None:
+                turns[a] = n % 2
+    groups = [[a for a in group if a is not None] for group in groups]
     shapes = [x.shape for x in ins]
-    total = sum(len(blocks_of(s[2:])) for s in shapes)
-    per = -(-total // deep)
+    pers = [-(-sum(len(blocks_of(shapes[a][2:])) for a in group) // deep) for group in groups]
+    many = len(groups)
     sems = pltpu.SemaphoreType.DMA
     vmem = lambda *s: pltpu.VMEM(s, jnp.bfloat16)
+    out_shapes = [
+        (layers, 2, g.shape[0] // shards // 2, g.shape[1]) for g in grads[0][:4]
+    ] + [(1,) + shapes[-1][1:]]
     outs = pl.pallas_call(
-        functools.partial(reduce_kernel, shards, deep, per, count),
-        out_shape=[jax.ShapeDtypeStruct(s[1:], jnp.float32) for s in shapes],
+        functools.partial(reduce_kernel, shards, deep, plan, groups, pers, turns),
+        out_shape=[jax.ShapeDtypeStruct(s, jnp.float32) for s in out_shapes],
         in_specs=[pl.BlockSpec(memory_space=pltpu.VMEM)] * count,
-        out_specs=[pl.BlockSpec(memory_space=pltpu.VMEM)] * count,
+        out_specs=[pl.BlockSpec(memory_space=pltpu.VMEM)] * len(out_shapes),
         scratch_shapes=[vmem(s[0], *s[2:]) for s in shapes]
-        + [vmem(s[0], *s[2:]) for s in shapes]
-        + [vmem(s[0] - 1, *s[2:]) for s in shapes]
+        + [vmem(3, *s[2:]) for s in shapes]
+        + [vmem(3, *s[2:]) for s in shapes]
+        + [vmem(deep, per, BLOCK, 128) for per in pers]
+        + [vmem(deep - 1, per, BLOCK, 128) for per in pers]
+        + [vmem(per, BLOCK, 128) for per in pers]
+        + [vmem(deep, per, BLOCK, 128) for per in pers]
+        + [vmem(deep, per, BLOCK, 128) for per in pers]
         + [
-            vmem(deep, per, BLOCK, 128), vmem(deep - 1, per, BLOCK, 128),
-            vmem(per, BLOCK, 128), vmem(deep, per, BLOCK, 128), vmem(deep, per, BLOCK, 128),
             sems((count,)), sems((count,)),
-            sems((count, shards - 1)), sems((count, shards - 1)),
-            sems((deep - 1,)), sems((deep - 1,)),
-            sems((deep - 1,)), sems((deep - 1,)),
-            sems((deep,)), sems((deep,)), sems((1,)),
+            sems((count, 2)), sems((count, 2)),
+            sems((many, deep - 1)), sems((many, deep - 1)),
+            sems((many, deep - 1)), sems((many, deep - 1)),
+            sems((many,)), sems((many,)), sems((many,)),
         ],
         compiler_params=pltpu.CompilerParams(
             collective_id=1, has_side_effects=True, vmem_limit_bytes=56 * 1024 * 1024
         ),
         name="reduce_grads",
     )(*ins)
-    big = [
-        jnp.stack([outs[layer * 4 + a].reshape(-1, shapes[a][3]) for layer in range(layers)], 0)
-        for a in range(4)
-    ]
-    tiny = outs[-1][:, :half, :width].reshape(layers, rows // layers, width)
+    big = [x.reshape(layers, -1, x.shape[3]) for x in outs[:4]]
+    tiny = outs[-1][0, :, :half, :width].reshape(layers, rows // layers, width)
     return tuple(big) + (
         tiny[:, :ng],
         tiny[:, ng : ng + nb],

time: 228 us -> 203 us (0.89)
  Pallas kernels: 138 us -> 115 us
  local copies, waits for them, and re-layouts: 22 us -> 28.9 us
  other arithmetic: 15.5 us -> 10.4 us
    pallas_call x1, Pallas kernels: 90.8 us -> 69.9 us  [reduce_all(): pl.pallas_call(functools.partial(reduce_kernel, shards, deep, plan, group...]
    another operation x4 -> x0, other arithmetic: 5.14 us -> none  [reduce_all(): jnp.stack([outs[layer * 4 + a].reshape(-1, shapes[a][3]) for layer in ran...]
    unnamed x103 -> x109, local copies, waits for them, and re-layouts: 8.13 us -> 13.1 us
    slice x0 -> x4, local copies, waits for them, and re-layouts: none -> 3.21 us  [the longest x2 1.71 us: reduce_all(): qkv[:, :cut]]
where the time goes in v2:
time: 203 us; the launch traced here: 202 us
  Pallas kernels  115 us (57%)
  matrix products  45.3 us (22%)
  local copies, waits for them, and re-layouts  28.9 us (14%)
  other arithmetic  10.4 us (5%)
    pallas_call x1, Pallas kernels, reduce_all(): pl.pallas_call(functools.partial(reduce_kernel, shards, deep, plan, group...  69.9 us
    pallas_call x1, Pallas kernels, gather(): pl.pallas_call(functools.partial(gather_kernel, shards, layers, count), o...  45.2 us
    dot_general x8, matrix products, product_left(): lax.dot_general(left, right, (((0,), (0,)), ((), ())), preferred_element_...  14 us
    dot_general x12, matrix products, batched(): return jnp.einsum(form, left, right, preferred_element_type=jnp.float32)  13.7 us
    unnamed x109, local copies, waits for them, and re-layouts  13.1 us
    dot_general x8, matrix products, product_right(): lax.dot_general(left, right, (((1,), (1,)), ((), ())), preferred_element_...  8.98 us
    dot_general x8, matrix products, product(): return jnp.dot(left, right, preferred_element_type=jnp.float32)  4.97 us

profile of v2, /device:TPU:0, one launch (start us, length us, event | category | flops | bytes accessed | tf_op | source)
XLA Modules:
  0.0 201.6 jit_solution(10997458126742303264)
XLA Ops:
  1.3 1.0 fusion.45
  2.4 2.0 reduce_sum.342
  4.4 1.2 multiply_reduce_fusion.13
  5.6 0.8 reshape.524
  6.4 0.7 copy.70
  7.1 1.3 fusion.90.refs_4_
  8.4 45.2 %gather_params.1 = (bf16[4,2,48,1152]{3,2,1,0:T(8,128)(2,1)}, bf16[4,2,48,384]{3,2,1,0:T(8,128)(2,1)}, bf16[4,2,48,1536]{3,2,1,0:T(8,128)(2,1)}, bf16[4,2,192,38...) custom-call(bf16[2,2,48,1152]{3,2,1,0:T(8,128)(2,1)} %bitcast.246, ...), custom_call_target="tpu_custom_call" | custom-call | tf_op jit(solution)/shard_map/gather_params/pallas_call | solution.py:289
  53.6 0.8 slice_bitcast_fusion.1
  56.0 0.5 add_convert_fusion.4
  58.0 0.5 convolution_convert_fusion.11
  58.5 0.5 copy-done.6
  59.7 0.7 copy-done.16
  60.3 1.6 multiply_convert_fusion.3
  62.0 0.6 fusion.109
  64.2 1.4 fusion.118
  65.6 2.2 %convolution_convert_fusion.10 = bf16[6,64,197]{2,1,0:T(8,128)(2,1)S(1)} fusion(bf16[197,6,64]{0,2,1:T(8,128)(2,1)S(1)} %bitcast.236, f32[6,197,197]{1,2,0:T(8,128)} %fusion.118), kind=kOutput, calls=%fused_computation.56 | convolution fusion | flops 30348046 | bytes 1234008 | tf_op jit(solution)/shard_map/bhqk,bkhe->bqhe/dot_general | solution.py:62
  68.5 0.7 copy-done.18
  69.2 0.6 multiply_convert_fusion.2
  70.5 0.8 fusion.116
  71.4 0.5 fusion.23
  71.9 1.0 copy.91
  72.9 1.3 multiply_reduce_fusion.2
  74.3 0.7 stack.71
  74.9 1.2 fusion.101
  76.1 1.9 convolution_convert_fusion.13
  78.2 1.7 copy.80
  80.0 3.0 %fusion.104 = (bf16[6,64]{1,0:T(8,128)(2,1)S(1)}, bf16[1,197,6,64]{1,3,2,0:T(8,128)(2,1)}) fusion(bf16[197,6,64]{0,2,1:T(8,128)(2,1)} %bitcast.242, f32[6,197,197]{1,2,0:T(8,128)} %fusion.118), kind=kOutput, calls=%fused_computation.224 | convolution fusion | flops 30423310 | bytes 1234776 | tf_op jit(solution)/shard_map/bhqk,bqhe->bkhe/dot_general | solution.py:62
  83.0 1.9 convolution_convert_fusion.7
  84.9 2.7 %convolution_convert_fusion.4 = bf16[384,1536]{1,0:T(8,128)(2,1)} fusion(bf16[197,1536]{1,0:T(8,128)(2,1)} %copy-done.36, f32[197,384]{1,0:T(8,128)S(1)} %get-tuple-element.123, f32[384]{0:T(512)S(1)} %add.255, f32[384]{0:T(512)S(1)} %mul.339, f32[197]{0:T(256)S(1)} %add_rsqrt_fusion, f32[197]{0:T(256)S(1)} %broadcast_multiply_fusion.8), kind=kOutput, calls=%fused_computation.6 | convolution fusion | flops 233358720 | bytes 2092072 | tf_op jit(solution)/shard_map/dot_general | solution.py:50
  87.6 1.8 convolution_convert_fusion.5
  89.8 3.0 %multiply_reduce_fusion.1 = (f32[6,197]{1,0:T(8,128)S(1)}, f32[6,197,197]{1,2,0:T(8,128)}) fusion(f32[6,197,197]{1,2,0:T(8,128)S(1)} %fusion.119, bf16[197,6,64]{0,2,1:T(8,128)(2,1)} %bitcast.201, bf16[197,6,64]{0,2,1:T(8,128)(2,1)} %bitcast.198), kind=kOutput, calls=%fused_computation.31 | convolution fusion | flops 60309384 | bytes 2170152 | tf_op jit(solution)/shard_map/reduce_sum | solution.py:82
  92.7 1.6 multiply_convert_fusion.1
  94.3 1.0 convolution_convert_fusion.9
  95.4 0.9 fusion.105
  96.4 2.4 %multiply_reduce_fusion.3 = (bf16[384]{0:T(512)(128)(2,1)S(1)}, f32[197]{0:T(256)S(1)}, f32[197]{0:T(256)S(1)}, bf16[384]{0:T(512)(128)(2,1)}, f32[197,384]{1,0:T(8,128)S(1)}) fusion(f32[197,384]{1,0:T(8,128)S(1)} %get-tuple-element.121, f32[197]{0:T(256)S(1)} %add_rsqrt_fusion.1, f32[197]{0:T(256)S(1)} %broadcast_multiply_fusion.9, f32[384]{0:T(512)S(1)} %mul.332, ...), kind=kOutput, calls=%fused_computation.83 | convolution fusion | flops 176334336 | bytes 1950032 | tf_op jit(solution)/shard_map/dot_general | solution.py:56
  98.8 0.6 stack.70
  99.6 2.7 %convolution_convert_fusion.3 = bf16[384,1152]{1,0:T(8,128)(2,1)} fusion(bf16[197,384]{0,1:T(8,128)(2,1)} %bitcast.261, bf16[197,384]{0,1:T(8,128)(2,1)} %bitcast.253, bf16[197,384]{0,1:T(8,128)(2,1)} %bitcast.255, f32[197,384]{1,0:T(8,128)S(1)} %get-tuple-element.121, f32[384]{0:T(512)S(1)} %add.241, f32[384]{0:T(512)S(1)} %mul.332, ...), kind=kOutput, calls=%fused_computation.5 | convolution fusion | flops 176475264 | bytes 1645864 | tf_op jit(solution)/shard_map/dot_general | solution.py:50
  102.3 0.8 fusion.115
  103.6 0.7 multiply_reduce_fusion.4
  104.4 0.6 stack.61
  105.7 0.6 stack.66
  106.8 3.0 %fusion.106 = (bf16[6,64]{1,0:T(8,128)(2,1)S(1)}, bf16[1,197,6,64]{1,3,2,0:T(8,128)(2,1)}) fusion(bf16[197,6,64]{0,2,1:T(8,128)(2,1)S(1)} %bitcast.240, f32[6,197,197]{1,2,0:T(8,128)} %copy-done.6), kind=kOutput, calls=%fused_computation.226 | convolution fusion | flops 30423310 | bytes 1234776 | tf_op jit(solution)/shard_map/bhqk,bqhe->bkhe/dot_general | solution.py:62
  109.8 1.0 convolution_convert_fusion.6
  110.8 1.7 convolution_convert_fusion.1
  112.5 1.6 convolution_convert_fusion.2
  114.1 0.7 slice.210
  114.8 0.9 slice.209
  116.1 0.7 multiply_reduce_fusion
  118.2 0.7 multiply_reduce_fusion.5
  119.2 1.0 copy.92
  120.5 0.7 pad.9.refs_10_
  121.2 0.6 convolution_convert_fusion
  121.8 0.8 slice.212
  122.5 0.9 slice.211
  123.4 69.9 %reduce_grads.1 = (f32[2,2,48,1152]{3,2,1,0:T(8,128)}, f32[2,2,48,384]{3,2,1,0:T(8,128)}, f32[2,2,48,1536]{3,2,1,0:T(8,128)}, f32[2,2,192,384]{3,2,1,0:T(8,128)}, f32[1,2,48,128]{3,2,1,0:T(8,128)}) custom-call(bf16[4,2,192,384]{3,2,1,0:T(8,128)(2,1)} %bitcast.204, bf16[4,2,48,1536]{3,2,1,0:T(8,128)(2,1)} %bitcast.203, bf16[4,2,48,768]{3,2,1,0:T(8,128)(2,1)} %bitcast.207, ...), custom_call_target="tpu_custom_call" | custom-call | tf_op jit(solution)/shard_map/reduce_grads/pallas_call | solution.py:509
  193.3 0.8 slice_bitcast_fusion
  194.1 0.6 slice.213
  194.7 0.6 copy.93
  195.3 0.7 reshape.565
  196.0 2.1 %copy.161 = f32[2,96,1152]{2,1,0:T(8,128)} copy(f32[2,96,1152]{2,1,0:T(8,128)} %bitcast.231) | data formatting | bytes 1769472
  198.1 0.7 copy.162
  198.8 1.0 copy.163
  199.9 0.7 copy-done.11
  200.5 1.0 copy.164
  (188 shorter events, 11.7 us)
Async XLA Ops:
  4.4 51.6 %copy-start = (f32[1,197,384]{2,0,1:T(1,128)S(1)}, f32[1,197,384]{2,0,1:T(1,128)}, u32[]{:S(2)}) copy-start(f32[1,197,384]{2,0,1:T(1,128)} %param.10) | copy-start | bytes 907780
  53.5 3.0 %copy-start.19 = (bf16[4,2,48,1152]{3,2,1,0:T(8,128)(2,1)S(1)}, bf16[4,2,48,1152]{3,2,1,0:T(8,128)(2,1)}, u32[]{:S(2)}) copy-start(bf16[4,2,48,1152]{3,2,1,0:T(8,128)(2,1)} %get-tuple-element.24) | copy-start | bytes 2654212
  57.5 0.9 copy-start.24
  57.5 1.4 copy-start.13
  57.9 1.0 copy-start.6
  59.0 0.7 copy-start.26
  59.0 1.3 copy-start.16
  60.3 1.6 copy-start.8
  62.0 1.2 copy-start.21
  63.8 3.9 %copy-start.3 = (bf16[197,384]{0,1:T(8,128)(2,1)}, bf16[197,384]{0,1:T(8,128)(2,1)S(1)}, u32[]{:S(2)}) copy-start(bf16[197,384]{0,1:T(8,128)(2,1)S(1)} %copy.76) | copy-start | bytes 453892
  64.0 3.8 %copy-start.1 = (bf16[197,384]{0,1:T(8,128)(2,1)}, bf16[197,384]{0,1:T(8,128)(2,1)S(1)}, u32[]{:S(2)}) copy-start(bf16[197,384]{0,1:T(8,128)(2,1)S(1)} %copy.77) | copy-start | bytes 453892
  64.2 3.6 %copy-start.28 = (bf16[197,384]{0,1:T(8,128)(2,1)}, bf16[197,384]{0,1:T(8,128)(2,1)S(1)}, u32[]{:S(2)}) copy-start(bf16[197,384]{0,1:T(8,128)(2,1)S(1)} %copy.75) | copy-start | bytes 453892
  64.2 3.7 %copy-start.15 = (bf16[4,2,48,384]{3,2,1,0:T(8,128)(2,1)S(1)}, bf16[4,2,48,384]{3,2,1,0:T(8,128)(2,1)}, u32[]{:S(2)}) copy-start(bf16[4,2,48,384]{3,2,1,0:T(8,128)(2,1)} %get-tuple-element.29) | copy-start | bytes 884740
  67.8 0.7 copy-start.30
  67.8 1.3 copy-start.18
  69.2 1.0 copy-start.5
  69.2 1.4 copy-start.10
  71.4 1.5 copy-start.36
  87.6 1.8 copy-start.29
  87.6 1.8 copy-start.33
  92.7 1.6 copy-start.4
  92.7 2.6 %copy-start.2 = (bf16[197,384]{0,1:T(8,128)(2,1)S(1)}, bf16[197,384]{0,1:T(8,128)(2,1)}, u32[]{:S(2)}) copy-start(bf16[197,384]{0,1:T(8,128)(2,1)} %copy-done.1) | copy-start | bytes 453892
  94.3 2.0 %copy-start.22 = (bf16[4,2,48,1152]{3,2,1,0:T(8,128)(2,1)S(1)}, bf16[4,2,48,1152]{3,2,1,0:T(8,128)(2,1)}, u32[]{:S(2)}) copy-start(bf16[4,2,48,1152]{3,2,1,0:T(8,128)(2,1)} %get-tuple-element.28) | copy-start | bytes 2654212
  99.4 2.9 %copy-start.9 = (bf16[4,2,192,384]{3,2,1,0:T(8,128)(2,1)S(1)}, bf16[4,2,192,384]{3,2,1,0:T(8,128)(2,1)}, u32[]{:S(2)}) copy-start(bf16[4,2,192,384]{3,2,1,0:T(8,128)(2,1)} %get-tuple-element.27) | copy-start | bytes 3538948
  99.6 2.8 %copy-start.7 = (f32[197,1536]{1,0:T(8,128)S(1)}, f32[197,1536]{1,0:T(8,128)}, u32[]{:S(2)}) copy-start(f32[197,1536]{1,0:T(8,128)} %get-tuple-element.119) | copy-start | bytes 3631108
  102.3 1.3 copy-start.17
  103.2 1.1 copy-start.34
  104.3 1.1 copy-start.14
  104.3 2.1 %copy-start.42 = (bf16[384]{0:T(512)(128)(2,1)S(1)}, bf16[384]{0:T(512)(128)(2,1)}, u32[]{:S(2)}) copy-start(bf16[384]{0:T(512)(128)(2,1)} %get-tuple-element.77) | copy-start | bytes 2308
  105.4 4.4 %copy-start.27 = (bf16[6,64,197]{2,1,0:T(8,128)(2,1)S(1)}, bf16[6,64,197]{2,1,0:T(8,128)(2,1)}, u32[]{:S(2)}) copy-start(bf16[6,64,197]{2,1,0:T(8,128)(2,1)} %copy-done.26) | copy-start | bytes 453892
  106.7 5.7 %copy-start.31 = (bf16[197,384]{0,1:T(8,128)(2,1)}, bf16[197,384]{0,1:T(8,128)(2,1)S(1)}, u32[]{:S(2)}) copy-start(bf16[197,384]{0,1:T(8,128)(2,1)S(1)} %copy.84) | copy-start | bytes 453892
  106.8 4.0 %copy-start.35 = (bf16[197,1536]{1,0:T(8,128)(2,1)S(1)}, bf16[197,1536]{1,0:T(8,128)(2,1)}, u32[]{:S(2)}) copy-start(bf16[197,1536]{1,0:T(8,128)(2,1)} %copy-done.34) | copy-start | bytes 1815556
  112.5 1.6 copy-start.23
  114.1 1.6 copy-start.25
  114.1 1.6 copy-start.32
  117.0 1.2 copy-start.20
  117.0 1.2 copy-start.43
  118.9 1.5 copy-start.38
  118.9 1.5 copy-start.41
  118.9 1.5 copy-start.39
  118.9 1.5 copy-start.40
  193.3 4.8 %copy-start.37 = (f32[2,2,48,384]{3,2,1,0:T(8,128)S(1)}, f32[2,2,48,384]{3,2,1,0:T(8,128)}, u32[]{:S(2)}) copy-start(f32[2,2,48,384]{3,2,1,0:T(8,128)} %get-tuple-element.33) | copy-start | bytes 884740
  193.3 5.5 %copy-start.12 = (f32[2,2,48,1536]{3,2,1,0:T(8,128)S(1)}, f32[2,2,48,1536]{3,2,1,0:T(8,128)}, u32[]{:S(2)}) copy-start(f32[2,2,48,1536]{3,2,1,0:T(8,128)} %get-tuple-element.34) | copy-start | bytes 3538948
  198.8 1.7 copy-start.11

commit v3 on v2

--- a/solution.py
+++ b/solution.py
@@ -191,83 +191,92 @@
 
 
 def gather_kernel(shards, layers, count, *refs):
-    ins = refs[: count + 1]
-    outs = refs[count + 1 : count + 2 + count * layers]
-    send, recv, psend, precv, ssend, srecv, local = refs[count + 2 + count * layers :]
+    ins, outs = refs[: count + 1], refs[count + 1 : 2 * count + 2]
+    send, recv, psend, precv, zsend, zrecv, qsend, qrecv, ssend, srecv, local = refs[2 * count + 2 :]
     me, rep, core, depth, mate = place(shards, 0)
+    odd = lax.rem(depth, 2)
+    across = (depth + 1 - 2 * odd) * 2 + core
+    side = (me + 1 - 2 * lax.rem(me, 2), lax.rem(me + 2, shards))
+    far = shards - 1 - me
     barrier = pltpu.get_barrier_semaphore()
     pl.semaphore_signal(barrier, inc=1, device_id=(me, mate), device_id_type=MESH)
+    pl.semaphore_signal(barrier, inc=1, device_id=(me, across), device_id_type=MESH)
     for k in range(1, shards):
         peer = lax.rem(me + k, shards)
         pl.semaphore_signal(barrier, inc=1, device_id=(peer, rep), device_id_type=MESH)
-    pl.semaphore_wait(barrier, shards)
-    small_in, small_out = ins[count], outs[count * layers]
+    pl.semaphore_wait(barrier, shards + 1)
+
+    started = []
+
+    def remote(src, dst, send_sem, recv_sem, device):
+        copy = pltpu.make_async_remote_copy(
+            src_ref=src, dst_ref=dst, send_sem=send_sem, recv_sem=recv_sem, device_id=device,
+            device_id_type=MESH)
+        copy.start()
+        started.append(copy)
+        return copy
+
+    small_in, small_out = ins[count], outs[count]
+    swapped = [(a, odd) for a in (2, 0, 1)]
+    items = swapped + [(3, layer) for layer in range(layers)]
+    first = []
+    for item, (a, layer) in enumerate(items):
+        for k in range(2):
+            first.append(remote(
+                ins[a].at[layer, core], outs[a].at[layer, me, core], send.at[item, k],
+                recv.at[item, k], (side[k], rep)))
     smalls = []
     for k in range(1, shards):
         peer = lax.rem(me + k, shards)
-        copy = pltpu.make_async_remote_copy(
-            src_ref=small_in, dst_ref=small_out.at[me], send_sem=ssend.at[k - 1],
-            recv_sem=srecv.at[k - 1], device_id=(peer, rep), device_id_type=MESH)
-        copy.start()
-        smalls.append(copy)
-    side = (me + 1 - 2 * lax.rem(me, 2), lax.rem(me + 2, shards))
-    items = layers * count
-    first = []
-    for layer in range(layers):
-        for a in range(count):
-            item = layer * count + a
-            for k in range(2):
-                copy = pltpu.make_async_remote_copy(
-                    src_ref=ins[a].at[layer, core], dst_ref=outs[item].at[me, core],
-                    send_sem=send.at[item, k], recv_sem=recv.at[item, k],
-                    device_id=(side[k], rep), device_id_type=MESH)
-                copy.start()
-                first.append(copy)
+        smalls.append(remote(
+            small_in, small_out.at[me], ssend.at[k - 1], srecv.at[k - 1], (peer, rep)))
     own = []
-    for layer in range(layers):
-        for a in range(count):
-            item = layer * count + a
-            copy = pltpu.make_async_copy(ins[a].at[layer], outs[item].at[me], local.at[item])
+    for a in range(count):
+        for layer in range(layers):
+            copy = pltpu.make_async_copy(
+                ins[a].at[layer], outs[a].at[layer, me], local.at[a * layers + layer])
             copy.start()
             own.append(copy)
     copy = pltpu.make_async_copy(small_in, small_out.at[me], local.at[layers * count])
     copy.start()
     own.append(copy)
-    second = []
-
-    def to_mate(item, slot, origin):
-        piece = outs[item].at[origin, core]
-        passed = pltpu.make_async_remote_copy(
-            src_ref=piece, dst_ref=piece, send_sem=psend.at[item, slot],
-            recv_sem=precv.at[item, slot], device_id=(me, mate), device_id_type=MESH)
-        passed.start()
-        second.append(passed)
-
-    relays = [None] * items
-    for item in range(items + 1):
-        if item < items:
-            via = (item + item // count) % 2
+    passed, crossed = [], []
+
+    def hand_on(item, slot, origin):
+        a, layer = items[item]
+        piece = outs[a].at[layer, origin, core]
+        if item < len(swapped):
+            copy = remote(piece, piece, zsend.at[item, slot], zrecv.at[item, slot], (me, across))
+            crossed.append((item, slot, origin, copy))
+        passed.append(
+            remote(piece, piece, psend.at[item, slot], precv.at[item, slot], (me, mate)))
+
+    relays = []
+    for item in range(len(items) + 1):
+        if item < len(items):
+            a, layer = items[item]
+            via = item % 2
             for k in (via, 1 - via):
                 first[2 * item + k].wait_recv()
                 if k == via:
-                    piece = outs[item].at[side[via], core]
-                    relays[item] = pltpu.make_async_remote_copy(
-                        src_ref=piece, dst_ref=piece, send_sem=send.at[item, 2],
-                        recv_sem=recv.at[item, 2], device_id=(side[1 - via], rep),
-                        device_id_type=MESH)
-                    relays[item].start()
-                to_mate(item, k, side[k])
+                    piece = outs[a].at[layer, side[via], core]
+                    relays.append(remote(
+                        piece, piece, send.at[item, 2], recv.at[item, 2], (side[1 - via], rep)))
+                hand_on(item, k, side[k])
         if item > 0:
             relays[item - 1].wait_recv()
-            to_mate(item - 1, 2, shards - 1 - me)
-    for copy in smalls:
-        copy.wait()
+            hand_on(item - 1, 2, far)
+    for item, slot, origin, copy in crossed:
+        copy.wait_recv()
+        piece = outs[items[item][0]].at[1 - odd, origin, core]
+        passed.append(
+            remote(piece, piece, qsend.at[item, slot], qrecv.at[item, slot], (me, mate)))
+    for copy in smalls + passed:
+        copy.wait_recv()
     for copy in own:
         copy.wait()
-    for copy in first + relays:
+    for copy in started:
         copy.wait_send()
-    for copy in second:
-        copy.wait()
 
 
 def gather(stacks, shards):
@@ -280,29 +289,25 @@
     rows = small.shape[1]
     small = jnp.pad(small, ((0, 0), (0, -rows % 16), (0, -width % 128)))
     count = len(ins)
-    shapes = [
-        jax.ShapeDtypeStruct((shards,) + w.shape[1:], w.dtype) for _ in range(layers) for w in ins
-    ]
+    shapes = [jax.ShapeDtypeStruct((layers, shards) + w.shape[1:], w.dtype) for w in ins]
     shapes.append(jax.ShapeDtypeStruct((shards,) + small.shape, small.dtype))
     sems = pltpu.SemaphoreType.DMA
-    items = layers * count
+    table = sems((count - 1 + layers, shards - 1))
+    cross = sems((count - 1, shards - 1))
     outs = pl.pallas_call(
         functools.partial(gather_kernel, shards, layers, count),
         out_shape=shapes,
         in_specs=[pl.BlockSpec(memory_space=pltpu.VMEM)] * (count + 1),
         out_specs=[pl.BlockSpec(memory_space=pl.ANY)] * len(shapes),
-        scratch_shapes=[
-            sems((items, shards - 1)), sems((items, shards - 1)),
-            sems((items, shards - 1)), sems((items, shards - 1)),
-            sems((shards - 1,)), sems((shards - 1,)), sems((items + 1,)),
-        ],
+        scratch_shapes=[table] * 4 + [cross] * 4
+        + [sems((shards - 1,)), sems((shards - 1,)), sems((layers * count + 1,))],
         compiler_params=pltpu.CompilerParams(collective_id=0, has_side_effects=True),
         name="gather_params",
     )(*ins, small)
     tiny = outs[-1][:, :, :rows, :width]
     params = []
     for layer in range(layers):
-        big = [outs[layer * count + a].reshape(-1, weights[a].shape[2]) for a in range(count)]
+        big = [outs[a][layer].reshape(-1, weights[a].shape[2]) for a in range(count)]
         part = tiny[:, layer]
         ng, nb = gains.shape[1], biases.shape[1]
         params.append(tuple(big) + (

time: 203 us -> 203 us (level)
  Pallas kernels: 115 us -> 106 us
  local copies, waits for them, and re-layouts: 28.9 us -> 37.7 us
    pallas_call x1, Pallas kernels: 45.2 us -> 34.4 us  [gather(): pl.pallas_call(functools.partial(gather_kernel, shards, layers, count), o...]
    slice x0 -> x4, local copies, waits for them, and re-layouts: none -> 6.27 us  [gather(): outs[a][layer].reshape(-1, weights[a].shape[2])]
    unnamed x109 -> x113, local copies, waits for them, and re-layouts: 13.1 us -> 13.7 us
where the time goes in v3:
time: 203 us; the launch traced here: 201 us
  Pallas kernels  106 us (52%)
  matrix products  44.8 us (22%)
  local copies, waits for them, and re-layouts  37.7 us (19%)
  other arithmetic  11 us (5%)
    pallas_call x1, Pallas kernels, reduce_all(): pl.pallas_call(functools.partial(reduce_kernel, shards, deep, plan, group...  71.4 us
    pallas_call x1, Pallas kernels, gather(): pl.pallas_call(functools.partial(gather_kernel, shards, layers, count), o...  34.4 us
    dot_general x8, matrix products, product_left(): lax.dot_general(left, right, (((0,), (0,)), ((), ())), preferred_element_...  14.1 us
    dot_general x12, matrix products, batched(): return jnp.einsum(form, left, right, preferred_element_type=jnp.float32)  13.7 us
    unnamed x113, local copies, waits for them, and re-layouts  13.7 us
    dot_general x8, matrix products, product_right(): lax.dot_general(left, right, (((1,), (1,)), ((), ())), preferred_element_...  8.42 us
    slice x4, local copies, waits for them, and re-layouts, gather(): outs[a][layer].reshape(-1, weights[a].shape[2])  6.27 us
    dot_general x8, matrix products, product(): return jnp.dot(left, right, preferred_element_type=jnp.float32)  4.97 us

profile of v3, /device:TPU:0, one launch (start us, length us, event | category | flops | bytes accessed | tf_op | source)
XLA Modules:
  0.0 201.4 jit_solution(15481305231695580385)
XLA Ops:
  1.3 1.0 fusion.45
  2.4 2.0 reduce_sum.342
  4.4 1.2 multiply_reduce_fusion.13
  5.6 0.8 reshape.500
  6.4 0.7 copy.70
  7.1 1.3 fusion.90.refs_4_
  8.4 34.4 %gather_params.1 = (bf16[2,4,2,48,1152]{4,3,2,1,0:T(8,128)(2,1)}, bf16[2,4,2,48,384]{4,3,2,1,0:T(8,128)(2,1)}, bf16[2,4,2,48,1536]{4,3,2,1,0:T(8,128)(2,1)}, bf1...) custom-call(bf16[2,2,48,1152]{3,2,1,0:T(8,128)(2,1)} %bitcast.246, bf16[2,2,48,384]{3,2,1,0:T(8,128)(2,1)} %bitcast.256, ...), custom_call_target="tpu_custom_call" | custom-call | tf_op jit(solution)/shard_map/gather_params/pallas_call | solution.py:297
  42.8 0.9 slice_bitcast_fusion.1
  45.9 1.1 fusion.107
  47.0 1.1 fusion.106
  51.1 2.8 %fusion.105 = (bf16[1,4,2,48,1536]{4,3,2,1,0:T(8,128)(2,1)}, bf16[1,4,2,48,1536]{4,3,2,1,0:T(8,128)(2,1)S(1)}) fusion(bf16[2,4,2,48,1536]{4,3,2,1,0:T(8,128)(2,1)} %get-tuple-element.22), kind=kLoop, calls=%fused_computation.225 | loop fusion | bytes 4718592 | tf_op jit(solution)/shard_map/slice | solution.py:310
  53.9 1.6 multiply_convert_fusion.3
  55.6 0.9 copy-done.21
  56.5 1.3 fusion.104
  59.8 0.7 slice.291
  60.5 0.7 fusion.27
  61.2 1.0 copy.76
  62.3 1.1 copy.77
  63.6 1.5 fusion.122
  65.0 2.2 %convolution_convert_fusion.10 = bf16[6,64,197]{2,1,0:T(8,128)(2,1)S(1)} fusion(bf16[197,6,64]{0,2,1:T(8,128)(2,1)S(1)} %bitcast.236, f32[6,197,197]{1,2,0:T(8,128)} %fusion.122), kind=kOutput, calls=%fused_computation.56 | convolution fusion | flops 30348046 | bytes 1234008 | tf_op jit(solution)/shard_map/bhqk,bkhe->bqhe/dot_general | solution.py:62
  67.9 0.7 copy-done.10
  69.2 0.7 copy-done.7
  69.9 0.8 fusion.120
  71.3 1.0 copy.91
  72.3 1.3 multiply_reduce_fusion.2
  73.7 0.6 stack.71
  74.3 1.2 fusion.101
  75.5 1.9 convolution_convert_fusion.13
  77.6 1.7 copy.80
  79.3 2.9 %fusion.108 = (bf16[6,64]{1,0:T(8,128)(2,1)S(1)}, bf16[1,197,6,64]{1,3,2,0:T(8,128)(2,1)}) fusion(bf16[197,6,64]{0,2,1:T(8,128)(2,1)} %bitcast.242, f32[6,197,197]{1,2,0:T(8,128)} %fusion.122), kind=kOutput, calls=%fused_computation.228 | convolution fusion | flops 30423310 | bytes 1234776 | tf_op jit(solution)/shard_map/bhqk,bqhe->bkhe/dot_general | solution.py:62
  82.4 1.9 convolution_convert_fusion.7
  84.3 2.9 %convolution_convert_fusion.4 = bf16[384,1536]{1,0:T(8,128)(2,1)} fusion(bf16[197,1536]{1,0:T(8,128)(2,1)} %copy-done.40, f32[197,384]{1,0:T(8,128)S(1)} %get-tuple-element.123, f32[384]{0:T(512)S(1)} %add.255, f32[384]{0:T(512)S(1)} %mul.339, f32[197]{0:T(256)S(1)} %add_rsqrt_fusion, f32[197]{0:T(256)S(1)} %broadcast_multiply_fusion.8), kind=kOutput, calls=%fused_computation.6 | convolution fusion | flops 233358720 | bytes 2092072 | tf_op jit(solution)/shard_map/dot_general | solution.py:50
  87.2 1.6 convolution_convert_fusion.5
  89.2 3.0 %multiply_reduce_fusion.1 = (f32[6,197]{1,0:T(8,128)S(1)}, f32[6,197,197]{1,2,0:T(8,128)}) fusion(f32[6,197,197]{1,2,0:T(8,128)S(1)} %fusion.123, bf16[197,6,64]{0,2,1:T(8,128)(2,1)} %bitcast.201, bf16[197,6,64]{0,2,1:T(8,128)(2,1)} %bitcast.198), kind=kOutput, calls=%fused_computation.31 | convolution fusion | flops 60309384 | bytes 2170152 | tf_op jit(solution)/shard_map/reduce_sum | solution.py:82
  92.1 1.6 multiply_convert_fusion.1
  93.8 1.0 convolution_convert_fusion.9
  94.8 0.9 fusion.109
  95.8 1.8 multiply_reduce_fusion.3
  97.6 0.7 stack.70
  98.5 2.8 %convolution_convert_fusion.3 = bf16[384,1152]{1,0:T(8,128)(2,1)} fusion(bf16[197,384]{0,1:T(8,128)(2,1)} %bitcast.261, bf16[197,384]{0,1:T(8,128)(2,1)} %bitcast.253, bf16[197,384]{0,1:T(8,128)(2,1)} %bitcast.255, f32[197,384]{1,0:T(8,128)S(1)} %get-tuple-element.121, f32[384]{0:T(512)S(1)} %add.241, f32[384]{0:T(512)S(1)} %mul.332, ...), kind=kOutput, calls=%fused_computation.5 | convolution fusion | flops 176475264 | bytes 1645864 | tf_op jit(solution)/shard_map/dot_general | solution.py:50
  101.3 0.8 fusion.119
  102.6 0.7 multiply_reduce_fusion.4
  103.4 0.6 stack.61
  105.2 3.0 %fusion.110 = (bf16[6,64]{1,0:T(8,128)(2,1)S(1)}, bf16[1,197,6,64]{1,3,2,0:T(8,128)(2,1)}) fusion(bf16[197,6,64]{0,2,1:T(8,128)(2,1)S(1)} %bitcast.240, f32[6,197,197]{1,2,0:T(8,128)} %copy-done.23), kind=kOutput, calls=%fused_computation.230 | convolution fusion | flops 30423310 | bytes 1234776 | tf_op jit(solution)/shard_map/bhqk,bqhe->bkhe/dot_general | solution.py:62
  108.2 1.0 convolution_convert_fusion.6
  109.2 1.6 convolution_convert_fusion.1
  110.8 1.6 convolution_convert_fusion.2
  112.4 0.7 slice.242
  113.2 0.9 slice.241
  114.4 0.7 multiply_reduce_fusion
  116.5 0.7 multiply_reduce_fusion.5
  117.6 1.0 copy.92
  118.9 0.6 pad.9.refs_10_
  120.1 0.8 slice.244
  120.8 0.9 slice.243
  121.7 71.4 %reduce_grads.1 = (f32[2,2,48,1152]{3,2,1,0:T(8,128)}, f32[2,2,48,384]{3,2,1,0:T(8,128)}, f32[2,2,48,1536]{3,2,1,0:T(8,128)}, f32[2,2,192,384]{3,2,1,0:T(8,128)}, f32[1,2,48,128]{3,2,1,0:T(8,128)}) custom-call(bf16[4,2,192,384]{3,2,1,0:T(8,128)(2,1)} %bitcast.204, bf16[4,2,48,1536]{3,2,1,0:T(8,128)(2,1)} %bitcast.203, bf16[4,2,48,768]{3,2,1,0:T(8,128)(2,1)} %bitcast.223, ...), custom_call_target="tpu_custom_call" | custom-call | tf_op jit(solution)/shard_map/reduce_grads/pallas_call | solution.py:514
  193.2 0.8 slice_bitcast_fusion
  194.6 0.6 copy.93
  195.2 0.7 reshape.533
  195.9 2.1 %copy.161 = f32[2,96,1152]{2,1,0:T(8,128)} copy(f32[2,96,1152]{2,1,0:T(8,128)} %bitcast.231) | data formatting | bytes 1769472
  198.0 0.7 copy.162
  198.7 1.0 copy.163
  199.7 0.7 copy-done.25
  200.4 1.0 copy.164
  (196 shorter events, 15.3 us)
Async XLA Ops:
  4.4 41.0 %copy-start = (f32[1,197,384]{2,0,1:T(1,128)S(1)}, f32[1,197,384]{2,0,1:T(1,128)}, u32[]{:S(2)}) copy-start(f32[1,197,384]{2,0,1:T(1,128)} %param.10) | copy-start | bytes 907780
  42.8 4.2 %copy-start.22 = (bf16[2,4,2,48,1152]{4,3,2,1,0:T(8,128)(2,1)S(1)}, bf16[2,4,2,48,1152]{4,3,2,1,0:T(8,128)(2,1)}, u32[]{:S(2)}) copy-start(bf16[2,4,2,48,1152]{4,3,2,1,0:T(8,128)(2,1)} %get-tuple-element.20) | copy-start | bytes 5308420
  47.0 3.4 %copy-start.18 = (bf16[1,4,2,48,384]{4,3,2,1,0:T(8,128)(2,1)}, bf16[1,4,2,48,384]{4,3,2,1,0:T(8,128)(2,1)S(1)}, u32[]{:S(2)}) copy-start(bf16[1,4,2,48,384]{4,3,2,1,0:T(8,128)(2,1)S(1)} %get-tuple-element.105) | copy-start | bytes 884740
  47.0 20.3 %copy-start.20 = (bf16[1,4,2,48,384]{4,3,2,1,0:T(8,128)(2,1)}, bf16[1,4,2,48,384]{4,3,2,1,0:T(8,128)(2,1)S(1)}, u32[]{:S(2)}) copy-start(bf16[1,4,2,48,384]{4,3,2,1,0:T(8,128)(2,1)S(1)} %get-tuple-element.104) | copy-start | bytes 884740
  48.1 0.9 copy-start.11
  49.5 0.9 copy-start.28
  49.9 1.1 copy-start.23
  50.4 0.7 copy-start.30
  53.9 1.6 copy-start.8
  53.9 2.5 %copy-start.21 = (bf16[2,4,2,192,384]{4,3,2,1,0:T(8,128)(2,1)S(1)}, bf16[2,4,2,192,384]{4,3,2,1,0:T(8,128)(2,1)}, u32[]{:S(2)}) copy-start(bf16[2,4,2,192,384]{4,3,2,1,0:T(8,128)(2,1)} %get-tuple-element.23) | copy-start | bytes 7077892
  57.8 1.0 copy-start.5
  57.8 1.6 copy-start.13
  62.3 4.9 %copy-start.3 = (bf16[197,384]{0,1:T(8,128)(2,1)}, bf16[197,384]{0,1:T(8,128)(2,1)S(1)}, u32[]{:S(2)}) copy-start(bf16[197,384]{0,1:T(8,128)(2,1)S(1)} %copy.76) | copy-start | bytes 453892
  63.4 3.8 %copy-start.1 = (bf16[197,384]{0,1:T(8,128)(2,1)}, bf16[197,384]{0,1:T(8,128)(2,1)S(1)}, u32[]{:S(2)}) copy-start(bf16[197,384]{0,1:T(8,128)(2,1)S(1)} %copy.77) | copy-start | bytes 453892
  63.6 3.7 %copy-start.32 = (bf16[197,384]{0,1:T(8,128)(2,1)}, bf16[197,384]{0,1:T(8,128)(2,1)S(1)}, u32[]{:S(2)}) copy-start(bf16[197,384]{0,1:T(8,128)(2,1)S(1)} %copy.75) | copy-start | bytes 453892
  67.2 0.7 copy-start.34
  67.2 1.3 copy-start.10
  68.6 1.3 copy-start.7
  68.6 1.3 copy-start.17
  70.7 1.5 copy-start.40
  87.2 1.6 copy-start.33
  87.2 1.6 copy-start.37
  92.1 1.6 copy-start.4
  92.1 2.6 %copy-start.2 = (bf16[197,384]{0,1:T(8,128)(2,1)S(1)}, bf16[197,384]{0,1:T(8,128)(2,1)}, u32[]{:S(2)}) copy-start(bf16[197,384]{0,1:T(8,128)(2,1)} %copy-done.1) | copy-start | bytes 453892
  93.7 2.0 %copy-start.14 = (bf16[1,4,2,48,1152]{4,3,2,1,0:T(8,128)(2,1)S(1)}, bf16[1,4,2,48,1152]{4,3,2,1,0:T(8,128)(2,1)}, u32[]{:S(2)}) copy-start(bf16[1,4,2,48,1152]{4,3,2,1,0:T(8,128)(2,1)} %get-tuple-element.98) | copy-start | bytes 2654212
  98.2 3.1 %copy-start.24 = (f32[197,1536]{1,0:T(8,128)S(1)}, f32[197,1536]{1,0:T(8,128)}, u32[]{:S(2)}) copy-start(f32[197,1536]{1,0:T(8,128)} %get-tuple-element.119) | copy-start | bytes 3631108
  98.4 3.7 %copy-start.15 = (f32[197,384]{1,0:T(8,128)}, f32[197,384]{1,0:T(8,128)S(1)}, u32[]{:S(2)}) copy-start(f32[197,384]{1,0:T(8,128)S(1)} %get-tuple-element.91) | copy-start | bytes 907780
  98.4 2.8 %copy-start.6 = (bf16[1,4,2,192,384]{4,3,2,1,0:T(8,128)(2,1)S(1)}, bf16[1,4,2,192,384]{4,3,2,1,0:T(8,128)(2,1)}, u32[]{:S(2)}) copy-start(bf16[1,4,2,192,384]{4,3,2,1,0:T(8,128)(2,1)} %copy-done.5) | copy-start | bytes 3538948
  101.3 1.3 copy-start.9
  102.1 1.1 copy-start.38
  102.6 1.6 copy-start.16
  103.3 1.1 copy-start.19
  104.4 3.8 %copy-start.31 = (bf16[6,64,197]{2,1,0:T(8,128)(2,1)S(1)}, bf16[6,64,197]{2,1,0:T(8,128)(2,1)}, u32[]{:S(2)}) copy-start(bf16[6,64,197]{2,1,0:T(8,128)(2,1)} %copy-done.30) | copy-start | bytes 453892
  105.1 4.0 %copy-start.35 = (bf16[197,384]{0,1:T(8,128)(2,1)}, bf16[197,384]{0,1:T(8,128)(2,1)S(1)}, u32[]{:S(2)}) copy-start(bf16[197,384]{0,1:T(8,128)(2,1)S(1)} %copy.84) | copy-start | bytes 453892
  105.1 4.0 %copy-start.39 = (bf16[197,1536]{1,0:T(8,128)(2,1)S(1)}, bf16[197,1536]{1,0:T(8,128)(2,1)}, u32[]{:S(2)}) copy-start(bf16[197,1536]{1,0:T(8,128)(2,1)} %copy-done.38) | copy-start | bytes 1815556
  110.8 1.6 copy-start.27
  112.4 1.6 copy-start.29
  112.4 1.6 copy-start.36
  115.3 1.2 copy-start.12
  115.4 1.2 copy-start.45
  117.2 1.5 copy-start.44
  117.2 1.5 copy-start.42
  117.3 1.5 copy-start.43
  193.2 4.8 %copy-start.41 = (f32[2,2,48,384]{3,2,1,0:T(8,128)S(1)}, f32[2,2,48,384]{3,2,1,0:T(8,128)}, u32[]{:S(2)}) copy-start(f32[2,2,48,384]{3,2,1,0:T(8,128)} %get-tuple-element.25) | copy-start | bytes 884740
  193.2 5.5 %copy-start.26 = (f32[2,2,48,1536]{3,2,1,0:T(8,128)S(1)}, f32[2,2,48,1536]{3,2,1,0:T(8,128)}, u32[]{:S(2)}) copy-start(f32[2,2,48,1536]{3,2,1,0:T(8,128)} %get-tuple-element.26) | copy-start | bytes 3538948
  198.7 1.7 copy-start.25

commit v4 on v3

--- a/solution.py
+++ b/solution.py
@@ -191,11 +191,13 @@
 
 
 def gather_kernel(shards, layers, count, *refs):
-    ins, outs = refs[: count + 1], refs[count + 1 : 2 * count + 2]
-    send, recv, psend, precv, zsend, zrecv, qsend, qrecv, ssend, srecv, local = refs[2 * count + 2 :]
+    ins, outs = refs[: count + 1], refs[count + 1 : count + 2 + layers * count]
+    send, recv, psend, precv, zsend, zrecv, qsend, qrecv, ssend, srecv, local = refs[
+        count + 2 + layers * count :
+    ]
     me, rep, core, depth, mate = place(shards, 0)
-    odd = lax.rem(depth, 2)
-    across = (depth + 1 - 2 * odd) * 2 + core
+    parity = lax.rem(depth, 2)
+    across = (depth + 1 - 2 * parity) * 2 + core
     side = (me + 1 - 2 * lax.rem(me, 2), lax.rem(me + 2, shards))
     far = shards - 1 - me
     barrier = pltpu.get_barrier_semaphore()
@@ -206,77 +208,81 @@
         pl.semaphore_signal(barrier, inc=1, device_id=(peer, rep), device_id_type=MESH)
     pl.semaphore_wait(barrier, shards + 1)
 
-    started = []
-
-    def remote(src, dst, send_sem, recv_sem, device):
-        copy = pltpu.make_async_remote_copy(
-            src_ref=src, dst_ref=dst, send_sem=send_sem, recv_sem=recv_sem, device_id=device,
-            device_id_type=MESH)
+    def work(odd):
+        started = []
+
+        def remote(src, dst, send_sem, recv_sem, device):
+            copy = pltpu.make_async_remote_copy(
+                src_ref=src, dst_ref=dst, send_sem=send_sem, recv_sem=recv_sem, device_id=device,
+                device_id_type=MESH)
+            copy.start()
+            started.append(copy)
+            return copy
+
+        small_in, small_out = ins[count], outs[layers * count]
+        swapped = [(a, odd) for a in (2, 0, 1)]
+        items = swapped + [(3, layer) for layer in range(layers)]
+        first = []
+        for item, (a, layer) in enumerate(items):
+            for k in range(2):
+                first.append(remote(
+                    ins[a].at[layer, core], outs[layer * count + a].at[me, core], send.at[item, k],
+                    recv.at[item, k], (side[k], rep)))
+        smalls = []
+        for k in range(1, shards):
+            peer = lax.rem(me + k, shards)
+            smalls.append(remote(
+                small_in, small_out.at[me], ssend.at[k - 1], srecv.at[k - 1], (peer, rep)))
+        own = []
+        for a in range(count):
+            for layer in range(layers):
+                copy = pltpu.make_async_copy(
+                    ins[a].at[layer], outs[layer * count + a].at[me], local.at[a * layers + layer])
+                copy.start()
+                own.append(copy)
+        copy = pltpu.make_async_copy(small_in, small_out.at[me], local.at[layers * count])
         copy.start()
-        started.append(copy)
-        return copy
-
-    small_in, small_out = ins[count], outs[count]
-    swapped = [(a, odd) for a in (2, 0, 1)]
-    items = swapped + [(3, layer) for layer in range(layers)]
-    first = []
-    for item, (a, layer) in enumerate(items):
-        for k in range(2):
-            first.append(remote(
-                ins[a].at[layer, core], outs[a].at[layer, me, core], send.at[item, k],
-                recv.at[item, k], (side[k], rep)))
-    smalls = []
-    for k in range(1, shards):
-        peer = lax.rem(me + k, shards)
-        smalls.append(remote(
-            small_in, small_out.at[me], ssend.at[k - 1], srecv.at[k - 1], (peer, rep)))
-    own = []
-    for a in range(count):
-        for layer in range(layers):
-            copy = pltpu.make_async_copy(
-                ins[a].at[layer], outs[a].at[layer, me], local.at[a * layers + layer])
-            copy.start()
-            own.append(copy)
-    copy = pltpu.make_async_copy(small_in, small_out.at[me], local.at[layers * count])
-    copy.start()
-    own.append(copy)
-    passed, crossed = [], []
-
-    def hand_on(item, slot, origin):
-        a, layer = items[item]
-        piece = outs[a].at[layer, origin, core]
-        if item < len(swapped):
-            copy = remote(piece, piece, zsend.at[item, slot], zrecv.at[item, slot], (me, across))
-            crossed.append((item, slot, origin, copy))
-        passed.append(
-            remote(piece, piece, psend.at[item, slot], precv.at[item, slot], (me, mate)))
-
-    relays = []
-    for item in range(len(items) + 1):
-        if item < len(items):
+        own.append(copy)
+        passed, crossed = [], []
+
+        def hand_on(item, slot, origin):
             a, layer = items[item]
-            via = item % 2
-            for k in (via, 1 - via):
-                first[2 * item + k].wait_recv()
-                if k == via:
-                    piece = outs[a].at[layer, side[via], core]
-                    relays.append(remote(
-                        piece, piece, send.at[item, 2], recv.at[item, 2], (side[1 - via], rep)))
-                hand_on(item, k, side[k])
-        if item > 0:
-            relays[item - 1].wait_recv()
-            hand_on(item - 1, 2, far)
-    for item, slot, origin, copy in crossed:
-        copy.wait_recv()
-        piece = outs[items[item][0]].at[1 - odd, origin, core]
-        passed.append(
-            remote(piece, piece, qsend.at[item, slot], qrecv.at[item, slot], (me, mate)))
-    for copy in smalls + passed:
-        copy.wait_recv()
-    for copy in own:
-        copy.wait()
-    for copy in started:
-        copy.wait_send()
+            piece = outs[layer * count + a].at[origin, core]
+            if item < len(swapped):
+                copy = remote(piece, piece, zsend.at[item, slot], zrecv.at[item, slot], (me, across))
+                crossed.append((item, slot, origin, copy))
+            passed.append(
+                remote(piece, piece, psend.at[item, slot], precv.at[item, slot], (me, mate)))
+
+        relays = []
+        for item in range(len(items) + 1):
+            if item < len(items):
+                a, layer = items[item]
+                via = item % 2
+                for k in (via, 1 - via):
+                    first[2 * item + k].wait_recv()
+                    if k == via:
+                        piece = outs[layer * count + a].at[side[via], core]
+                        relays.append(remote(
+                            piece, piece, send.at[item, 2], recv.at[item, 2], (side[1 - via], rep)))
+                    hand_on(item, k, side[k])
+            if item > 0:
+                relays[item - 1].wait_recv()
+                hand_on(item - 1, 2, far)
+        for item, slot, origin, copy in crossed:
+            copy.wait_recv()
+            piece = outs[(1 - odd) * count + items[item][0]].at[origin, core]
+            passed.append(
+                remote(piece, piece, qsend.at[item, slot], qrecv.at[item, slot], (me, mate)))
+        for copy in smalls + passed:
+            copy.wait_recv()
+        for copy in own:
+            copy.wait()
+        for copy in started:
+            copy.wait_send()
+
+    for odd in range(2):
+        pl.when(parity == odd)(functools.partial(work, odd))
 
 
 def gather(stacks, shards):
@@ -289,7 +295,9 @@
     rows = small.shape[1]
     small = jnp.pad(small, ((0, 0), (0, -rows % 16), (0, -width % 128)))
     count = len(ins)
-    shapes = [jax.ShapeDtypeStruct((layers, shards) + w.shape[1:], w.dtype) for w in ins]
+    shapes = [
+        jax.ShapeDtypeStruct((shards,) + w.shape[1:], w.dtype) for _ in range(layers) for w in ins
+    ]
     shapes.append(jax.ShapeDtypeStruct((shards,) + small.shape, small.dtype))
     sems = pltpu.SemaphoreType.DMA
     table = sems((count - 1 + layers, shards - 1))
@@ -307,7 +315,7 @@
     tiny = outs[-1][:, :, :rows, :width]
     params = []
     for layer in range(layers):
-        big = [outs[a][layer].reshape(-1, weights[a].shape[2]) for a in range(count)]
+        big = [outs[layer * count + a].reshape(-1, weights[a].shape[2]) for a in range(count)]
         part = tiny[:, layer]
         ng, nb = gains.shape[1], biases.shape[1]
         params.append(tuple(big) + (

time: 203 us -> 193 us (0.951)
  local copies, waits for them, and re-layouts: 37.7 us -> 28.9 us
    slice x4 -> x0, local copies, waits for them, and re-layouts: 6.27 us -> none  [gather(): outs[a][layer].reshape(-1, weights[a].shape[2])]
    unnamed x113 -> x109, local copies, waits for them, and re-layouts: 13.7 us -> 13.1 us
where the time goes in v4:
time: 193 us; the launch traced here: 192 us
  Pallas kernels  106 us (55%)
  matrix products  45.3 us (23%)
  local copies, waits for them, and re-layouts  28.9 us (15%)
  other arithmetic  10.4 us (5%)
  between operations  1.93 us (1%)
    pallas_call x1, Pallas kernels, reduce_all(): pl.pallas_call(functools.partial(reduce_kernel, shards, deep, plan, group...  71.5 us
    pallas_call x1, Pallas kernels, gather(): pl.pallas_call(functools.partial(gather_kernel, shards, layers, count), o...  34.4 us
    dot_general x8, matrix products, product_left(): lax.dot_general(left, right, (((0,), (0,)), ((), ())), preferred_element_...  13.8 us
    dot_general x12, matrix products, batched(): return jnp.einsum(form, left, right, preferred_element_type=jnp.float32)  13.7 us
    unnamed x109, local copies, waits for them, and re-layouts  13.1 us
    dot_general x8, matrix products, product_right(): lax.dot_general(left, right, (((1,), (1,)), ((), ())), preferred_element_...  9.16 us
    dot_general x8, matrix products, product(): return jnp.dot(left, right, preferred_element_type=jnp.float32)  4.96 us

profile of v4, /device:TPU:0, one launch (start us, length us, event | category | flops | bytes accessed | tf_op | source)
XLA Modules:
  0.0 192.4 jit_solution(5228236429603247230)
XLA Ops:
  1.3 1.0 fusion.45
  2.4 2.0 %reduce_sum.342 = f32[197]{0:T(256)S(1)} reduce(f32[1,197,384]{2,0,1:T(1,128)} %param.10, f32[]{:T(128)} %constant.29.clone.1), dimensions={0,2}, to_apply=%region_0.1 | reduce | flops 75451 | bytes 303384 | tf_op jit(solution)/shard_map/reduce_sum | solution.py:23
  4.4 1.2 multiply_reduce_fusion.13
  5.6 0.8 reshape.524
  6.4 0.7 copy.70
  7.1 1.3 fusion.90.refs_4_
  8.4 34.4 %gather_params.1 = (bf16[4,2,48,1152]{3,2,1,0:T(8,128)(2,1)}, bf16[4,2,48,384]{3,2,1,0:T(8,128)(2,1)}, bf16[4,2,48,1536]{3,2,1,0:T(8,128)(2,1)}, bf16[4,2,192,38...) custom-call(bf16[2,2,48,1152]{3,2,1,0:T(8,128)(2,1)} %bitcast.246, ...), custom_call_target="tpu_custom_call" | custom-call | tf_op jit(solution)/shard_map/gather_params/pallas_call | solution.py:305
  42.8 0.8 slice_bitcast_fusion.1
  45.3 0.5 add_convert_fusion.4
  47.2 0.5 convolution_convert_fusion.11
  47.7 0.5 copy-done.6
  48.9 0.7 copy-done.16
  49.6 1.6 multiply_convert_fusion.3
  51.2 0.6 fusion.109
  53.4 1.4 fusion.118
  54.9 2.2 %convolution_convert_fusion.10 = bf16[6,64,197]{2,1,0:T(8,128)(2,1)S(1)} fusion(bf16[197,6,64]{0,2,1:T(8,128)(2,1)S(1)} %bitcast.236, f32[6,197,197]{1,2,0:T(8,128)} %fusion.118), kind=kOutput, calls=%fused_computation.56 | convolution fusion | flops 30348046 | bytes 1234008 | tf_op jit(solution)/shard_map/bhqk,bkhe->bqhe/dot_general | solution.py:62
  57.7 0.7 copy-done.18
  58.4 0.6 multiply_convert_fusion.2
  59.8 0.8 fusion.116
  60.6 0.5 fusion.23
  61.1 1.0 copy.91
  62.2 1.3 multiply_reduce_fusion.2
  63.5 0.7 stack.71
  64.2 1.2 fusion.101
  65.4 1.9 %convolution_convert_fusion.13 = bf16[197,384]{1,0:T(8,128)(2,1)} fusion(bf16[384,384]{1,0:T(8,128)(2,1)} %bitcast.221, f32[197,384]{1,0:T(8,128)S(1)} %get-tuple-element.97), kind=kOutput, calls=%fused_computation.59 | convolution fusion | flops 58248960 | bytes 748800 | tf_op jit(solution)/shard_map/dot_general | solution.py:56
  67.5 1.7 copy.80
  69.2 3.0 %fusion.104 = (bf16[6,64]{1,0:T(8,128)(2,1)S(1)}, bf16[1,197,6,64]{1,3,2,0:T(8,128)(2,1)}) fusion(bf16[197,6,64]{0,2,1:T(8,128)(2,1)} %bitcast.242, f32[6,197,197]{1,2,0:T(8,128)} %fusion.118), kind=kOutput, calls=%fused_computation.224 | convolution fusion | flops 30423310 | bytes 1234776 | tf_op jit(solution)/shard_map/bhqk,bqhe->bkhe/dot_general | solution.py:62
  72.3 1.9 convolution_convert_fusion.7
  74.2 2.7 %convolution_convert_fusion.4 = bf16[384,1536]{1,0:T(8,128)(2,1)} fusion(bf16[197,1536]{1,0:T(8,128)(2,1)} %copy-done.36, f32[197,384]{1,0:T(8,128)S(1)} %get-tuple-element.123, f32[384]{0:T(512)S(1)} %add.255, f32[384]{0:T(512)S(1)} %mul.339, f32[197]{0:T(256)S(1)} %add_rsqrt_fusion, f32[197]{0:T(256)S(1)} %broadcast_multiply_fusion.8), kind=kOutput, calls=%fused_computation.6 | convolution fusion | flops 233358720 | bytes 2092072 | tf_op jit(solution)/shard_map/dot_general | solution.py:50
  76.9 1.6 convolution_convert_fusion.5
  78.9 3.0 %multiply_reduce_fusion.1 = (f32[6,197]{1,0:T(8,128)S(1)}, f32[6,197,197]{1,2,0:T(8,128)}) fusion(f32[6,197,197]{1,2,0:T(8,128)S(1)} %fusion.119, bf16[197,6,64]{0,2,1:T(8,128)(2,1)} %bitcast.201, bf16[197,6,64]{0,2,1:T(8,128)(2,1)} %bitcast.198), kind=kOutput, calls=%fused_computation.31 | convolution fusion | flops 60309384 | bytes 2170152 | tf_op jit(solution)/shard_map/reduce_sum | solution.py:82
  81.8 1.6 multiply_convert_fusion.1
  83.4 1.0 convolution_convert_fusion.9
  84.5 0.9 fusion.105
  85.5 2.5 %multiply_reduce_fusion.3 = (bf16[384]{0:T(512)(128)(2,1)S(1)}, f32[197]{0:T(256)S(1)}, f32[197]{0:T(256)S(1)}, bf16[384]{0:T(512)(128)(2,1)}, f32[197,384]{1,0:T(8,128)S(1)}) fusion(f32[197,384]{1,0:T(8,128)S(1)} %get-tuple-element.121, f32[197]{0:T(256)S(1)} %add_rsqrt_fusion.1, f32[197]{0:T(256)S(1)} %broadcast_multiply_fusion.9, f32[384]{0:T(512)S(1)} %mul.332, ...), kind=kOutput, calls=%fused_computation.83 | convolution fusion | flops 176334336 | bytes 1950032 | tf_op jit(solution)/shard_map/dot_general | solution.py:56
  88.0 0.6 stack.70
  88.9 2.7 %convolution_convert_fusion.3 = bf16[384,1152]{1,0:T(8,128)(2,1)} fusion(bf16[197,384]{0,1:T(8,128)(2,1)} %bitcast.261, bf16[197,384]{0,1:T(8,128)(2,1)} %bitcast.253, bf16[197,384]{0,1:T(8,128)(2,1)} %bitcast.255, f32[197,384]{1,0:T(8,128)S(1)} %get-tuple-element.121, f32[384]{0:T(512)S(1)} %add.241, f32[384]{0:T(512)S(1)} %mul.332, ...), kind=kOutput, calls=%fused_computation.5 | convolution fusion | flops 176475264 | bytes 1645864 | tf_op jit(solution)/shard_map/dot_general | solution.py:50
  91.6 0.8 fusion.115
  92.9 0.7 multiply_reduce_fusion.4
  93.7 0.6 stack.61
  95.0 0.6 stack.66
  96.0 3.0 %fusion.106 = (bf16[6,64]{1,0:T(8,128)(2,1)S(1)}, bf16[1,197,6,64]{1,3,2,0:T(8,128)(2,1)}) fusion(bf16[197,6,64]{0,2,1:T(8,128)(2,1)S(1)} %bitcast.240, f32[6,197,197]{1,2,0:T(8,128)} %copy-done.6), kind=kOutput, calls=%fused_computation.226 | convolution fusion | flops 30423310 | bytes 1234776 | tf_op jit(solution)/shard_map/bhqk,bqhe->bkhe/dot_general | solution.py:62
  99.1 1.0 convolution_convert_fusion.6
  100.1 1.7 convolution_convert_fusion.1
  101.7 1.6 convolution_convert_fusion.2
  103.4 0.7 slice.210
  104.1 0.9 slice.209
  105.4 0.7 multiply_reduce_fusion
  107.5 0.7 multiply_reduce_fusion.5
  108.5 1.0 copy.92
  109.8 0.7 pad.9.refs_10_
  110.5 0.6 convolution_convert_fusion
  111.0 0.8 slice.212
  111.8 0.9 slice.211
  112.6 71.5 %reduce_grads.1 = (f32[2,2,48,1152]{3,2,1,0:T(8,128)}, f32[2,2,48,384]{3,2,1,0:T(8,128)}, f32[2,2,48,1536]{3,2,1,0:T(8,128)}, f32[2,2,192,384]{3,2,1,0:T(8,128)}, f32[1,2,48,128]{3,2,1,0:T(8,128)}) custom-call(bf16[4,2,192,384]{3,2,1,0:T(8,128)(2,1)} %bitcast.204, bf16[4,2,48,1536]{3,2,1,0:T(8,128)(2,1)} %bitcast.203, bf16[4,2,48,768]{3,2,1,0:T(8,128)(2,1)} %bitcast.207, ...), custom_call_target="tpu_custom_call" | custom-call | tf_op jit(solution)/shard_map/reduce_grads/pallas_call | solution.py:522
  184.2 0.8 slice_bitcast_fusion
  185.0 0.6 slice.213
  185.6 0.6 copy.93
  186.2 0.7 reshape.565
  186.9 2.1 %copy.161 = f32[2,96,1152]{2,1,0:T(8,128)} copy(f32[2,96,1152]{2,1,0:T(8,128)} %bitcast.231) | data formatting | bytes 1769472
  189.0 0.7 copy.162
  189.7 1.0 copy.163
  190.7 0.7 copy-done.11
  191.4 1.0 copy.164
  (188 shorter events, 11.7 us)
Async XLA Ops:
  4.4 40.9 %copy-start = (f32[1,197,384]{2,0,1:T(1,128)S(1)}, f32[1,197,384]{2,0,1:T(1,128)}, u32[]{:S(2)}) copy-start(f32[1,197,384]{2,0,1:T(1,128)} %param.10) | copy-start | bytes 907780
  42.8 3.0 %copy-start.19 = (bf16[4,2,48,1152]{3,2,1,0:T(8,128)(2,1)S(1)}, bf16[4,2,48,1152]{3,2,1,0:T(8,128)(2,1)}, u32[]{:S(2)}) copy-start(bf16[4,2,48,1152]{3,2,1,0:T(8,128)(2,1)} %get-tuple-element.24) | copy-start | bytes 2654212
  46.8 0.9 copy-start.24
  46.8 1.4 copy-start.13
  47.2 1.0 copy-start.6
  48.2 0.7 copy-start.26
  48.2 1.3 copy-start.16
  49.6 1.6 copy-start.8
  51.2 1.2 copy-start.21
  53.1 3.9 %copy-start.3 = (bf16[197,384]{0,1:T(8,128)(2,1)}, bf16[197,384]{0,1:T(8,128)(2,1)S(1)}, u32[]{:S(2)}) copy-start(bf16[197,384]{0,1:T(8,128)(2,1)S(1)} %copy.76) | copy-start | bytes 453892
  53.3 3.8 %copy-start.1 = (bf16[197,384]{0,1:T(8,128)(2,1)}, bf16[197,384]{0,1:T(8,128)(2,1)S(1)}, u32[]{:S(2)}) copy-start(bf16[197,384]{0,1:T(8,128)(2,1)S(1)} %copy.77) | copy-start | bytes 453892
  53.4 3.6 %copy-start.28 = (bf16[197,384]{0,1:T(8,128)(2,1)}, bf16[197,384]{0,1:T(8,128)(2,1)S(1)}, u32[]{:S(2)}) copy-start(bf16[197,384]{0,1:T(8,128)(2,1)S(1)} %copy.75) | copy-start | bytes 453892
  53.4 3.7 %copy-start.15 = (bf16[4,2,48,384]{3,2,1,0:T(8,128)(2,1)S(1)}, bf16[4,2,48,384]{3,2,1,0:T(8,128)(2,1)}, u32[]{:S(2)}) copy-start(bf16[4,2,48,384]{3,2,1,0:T(8,128)(2,1)} %get-tuple-element.29) | copy-start | bytes 884740
  57.1 0.7 copy-start.30
  57.1 1.3 copy-start.18
  58.4 1.0 copy-start.5
  58.4 1.4 copy-start.10
  60.6 1.5 copy-start.36
  76.9 1.6 copy-start.29
  76.9 1.6 copy-start.33
  81.8 1.6 copy-start.4
  81.8 2.6 %copy-start.2 = (bf16[197,384]{0,1:T(8,128)(2,1)S(1)}, bf16[197,384]{0,1:T(8,128)(2,1)}, u32[]{:S(2)}) copy-start(bf16[197,384]{0,1:T(8,128)(2,1)} %copy-done.1) | copy-start | bytes 453892
  83.4 2.0 %copy-start.22 = (bf16[4,2,48,1152]{3,2,1,0:T(8,128)(2,1)S(1)}, bf16[4,2,48,1152]{3,2,1,0:T(8,128)(2,1)}, u32[]{:S(2)}) copy-start(bf16[4,2,48,1152]{3,2,1,0:T(8,128)(2,1)} %get-tuple-element.28) | copy-start | bytes 2654212
  88.7 2.9 %copy-start.9 = (bf16[4,2,192,384]{3,2,1,0:T(8,128)(2,1)S(1)}, bf16[4,2,192,384]{3,2,1,0:T(8,128)(2,1)}, u32[]{:S(2)}) copy-start(bf16[4,2,192,384]{3,2,1,0:T(8,128)(2,1)} %get-tuple-element.27) | copy-start | bytes 3538948
  88.9 2.8 %copy-start.7 = (f32[197,1536]{1,0:T(8,128)S(1)}, f32[197,1536]{1,0:T(8,128)}, u32[]{:S(2)}) copy-start(f32[197,1536]{1,0:T(8,128)} %get-tuple-element.119) | copy-start | bytes 3631108
  91.6 1.3 copy-start.17
  92.5 1.1 copy-start.34
  93.6 1.1 copy-start.14
  93.6 2.1 %copy-start.42 = (bf16[384]{0:T(512)(128)(2,1)S(1)}, bf16[384]{0:T(512)(128)(2,1)}, u32[]{:S(2)}) copy-start(bf16[384]{0:T(512)(128)(2,1)} %get-tuple-element.77) | copy-start | bytes 2308
  94.7 4.4 %copy-start.27 = (bf16[6,64,197]{2,1,0:T(8,128)(2,1)S(1)}, bf16[6,64,197]{2,1,0:T(8,128)(2,1)}, u32[]{:S(2)}) copy-start(bf16[6,64,197]{2,1,0:T(8,128)(2,1)} %copy-done.26) | copy-start | bytes 453892
  96.0 5.7 %copy-start.31 = (bf16[197,384]{0,1:T(8,128)(2,1)}, bf16[197,384]{0,1:T(8,128)(2,1)S(1)}, u32[]{:S(2)}) copy-start(bf16[197,384]{0,1:T(8,128)(2,1)S(1)} %copy.84) | copy-start | bytes 453892
  96.0 4.0 %copy-start.35 = (bf16[197,1536]{1,0:T(8,128)(2,1)S(1)}, bf16[197,1536]{1,0:T(8,128)(2,1)}, u32[]{:S(2)}) copy-start(bf16[197,1536]{1,0:T(8,128)(2,1)} %copy-done.34) | copy-start | bytes 1815556
  101.7 1.6 copy-start.23
  103.4 1.6 copy-start.25
  103.4 1.6 copy-start.32
  106.3 1.2 copy-start.20
  106.3 1.2 copy-start.43
  108.2 1.5 copy-start.38
  108.2 1.5 copy-start.41
  108.2 1.5 copy-start.39
  108.2 1.5 copy-start.40
  184.2 4.8 %copy-start.37 = (f32[2,2,48,384]{3,2,1,0:T(8,128)S(1)}, f32[2,2,48,384]{3,2,1,0:T(8,128)}, u32[]{:S(2)}) copy-start(f32[2,2,48,384]{3,2,1,0:T(8,128)} %get-tuple-element.33) | copy-start | bytes 884740
  184.2 5.5 %copy-start.12 = (f32[2,2,48,1536]{3,2,1,0:T(8,128)S(1)}, f32[2,2,48,1536]{3,2,1,0:T(8,128)}, u32[]{:S(2)}) copy-start(f32[2,2,48,1536]{3,2,1,0:T(8,128)} %get-tuple-element.34) | copy-start | bytes 3538948
  189.7 1.7 copy-start.11
